TPU v7x, 256 devices: a whole 4x4x8 slice. The times are simulated.
256 devices in a mesh: level: 2 (over core), blk: 128 (over z, x, y).
Axes of the slice: x: 4, y: 4, z: 8, core: 2. Of those that a mesh axis runs over, the one named last changes fastest.
Arguments:
- fluid_state: float32 [2, 2048, 5, 16, 256], P('level', 'blk'), may hold values from -0.5 to 4, as said below
- neighbours: int32 [2048, 6], replicated, may hold values from 0 to 2047, as said below
- parents: int32 [2048, 2], replicated, may hold values from 0 to 2047, as said below
Outputs:
- updated: float32 [2, 2048, 5, 16, 256], P('level', 'blk')
Inputs may be any that keep to these rules, and one draw needn't show every extreme that they name: Row b lists the coarse blocks beyond block b's low and high face along x, then y, then z; the relation is symmetric (the block beyond b's high face along an axis has b beyond its low face along it); block g is held by blk index g // 16, never by the same device as its neighbours; among the (block, face) pairs of one device at most 2 have their neighbour on any one other device, and some pairs of devices reach 2; no block beside a parent is a parent. `parents`: row g gives the coarse parent of refined block g and g's octant in it (4 x half + 2 y half + z half); the parent is held by the same blk index as g; every parent has one child of each octant, so each device's refined blocks are the children of 2 of its coarse blocks. `fluid_state`: components are density, x, y, z momentum and total energy of states with density 0.6 to 1.6, velocity components -0.3 to 0.3 and pressure 0.7 to 1.4, gamma 1.4.
All inputs are finite; a program needn't handle non-finite values.
Results may differ from a plain program's by a relative error of at most 0.0003.
Values sent between devices are 32-bit elements; how exact they have to be, the bound alone decides.
A program may use at most 192 MiB of HBM per device.

v0:
```python
import math

import jax
import jax.numpy as jnp
from jax import lax
from jax.sharding import PartitionSpec as P

GAS_GAMMA = 1.4
STEP_RATIO = 0.12
OPPOSITE = (1, 0, 3, 2, 5, 4)
FACE_SIGNS = (-1.0, 1.0, -1.0, 1.0, -1.0, 1.0)
BIT_OF = (4, 2, 1)
TANGENT = ((2, 1), (4, 1), (4, 2))


def shifted(array, axis, by):
    devices = lax.axis_size(axis)
    pairs = [(i, i + by) for i in range(devices) if 0 <= i + by < devices]
    return lax.ppermute(array, axis, pairs)


def primitive(state_vec):
    density = state_vec[0]
    velocity = state_vec[1:4] / density
    pressure = (GAS_GAMMA - 1.0) * (state_vec[4] - 0.5 * jnp.sum(state_vec[1:4] * velocity, axis=0))
    return (density, velocity, pressure)


def physical_flux(state_vec, normal, density, velocity, pressure):
    normal_speed = velocity[normal]
    pieces = [state_vec[component] * normal_speed for component in range(4)]
    pieces.append((state_vec[4] + pressure) * normal_speed)
    pieces[1 + normal] = pieces[1 + normal] + pressure
    return jnp.stack(pieces)


def contact_flux(low_state, high_state, normal):
    density_low, velocity_low, pressure_low = primitive(low_state)
    density_high, velocity_high, pressure_high = primitive(high_state)
    sound_low = jnp.sqrt(GAS_GAMMA * pressure_low / density_low)
    sound_high = jnp.sqrt(GAS_GAMMA * pressure_high / density_high)
    speed_low = velocity_low[normal]
    speed_high = velocity_high[normal]
    slowest = jnp.minimum(speed_low - sound_low, speed_high - sound_high)
    fastest = jnp.maximum(speed_low + sound_low, speed_high + sound_high)
    mass_low = density_low * (slowest - speed_low)
    mass_high = density_high * (fastest - speed_high)
    contact = (pressure_high - pressure_low + speed_low * mass_low - speed_high * mass_high) / (
        mass_low - mass_high
    )
    flux_low = physical_flux(low_state, normal, density_low, velocity_low, pressure_low)
    flux_high = physical_flux(high_state, normal, density_high, velocity_high, pressure_high)

    def star_flux(state_vec, density, velocity, pressure, mass_flow, wave_speed, flux_here):
        factor = mass_flow / (wave_speed - contact)
        momenta = [factor * velocity[component] for component in range(3)]
        momenta[normal] = factor * contact
        energy = factor * (
            state_vec[4] / density + (contact - velocity[normal]) * (contact + pressure / mass_flow)
        )
        star_state = jnp.stack([factor] + momenta + [energy])
        return flux_here + wave_speed * (star_state - state_vec)

    star_low = star_flux(
        low_state, density_low, velocity_low, pressure_low, mass_low, slowest, flux_low
    )
    star_high = star_flux(
        high_state, density_high, velocity_high, pressure_high, mass_high, fastest, flux_high
    )
    return jnp.where(
        slowest >= 0.0,
        flux_low,
        jnp.where(contact >= 0.0, star_low, jnp.where(fastest > 0.0, star_high, flux_high)),
    )


def face_fluxes(padded, normal):
    step_below = padded[:, :, 1:-1] - padded[:, :, :-2]
    step_above = padded[:, :, 2:] - padded[:, :, 1:-1]
    limited = jnp.where(
        step_below * step_above > 0.0,
        jnp.sign(step_below) * jnp.minimum(jnp.abs(step_below), jnp.abs(step_above)),
        0.0,
    )
    centre = padded[:, :, 1:-1]
    low_face = centre - 0.5 * limited
    high_face = centre + 0.5 * limited
    change = (
        0.5
        * STEP_RATIO
        * (
            physical_flux(low_face, normal, *primitive(low_face))
            - physical_flux(high_face, normal, *primitive(high_face))
        )
    )
    low_face = low_face + change
    high_face = high_face + change
    return contact_flux(high_face[:, :, :-1], low_face[:, :, 1:], normal)


def oriented(block_cells, direction):
    leading = block_cells.shape[:2]
    edge_cells = block_cells.shape[2]
    cube_cells = block_cells.reshape(leading + (edge_cells, edge_cells, edge_cells))
    if direction == 1:
        cube_cells = cube_cells.transpose(0, 1, 3, 2, 4)
    elif direction == 2:
        cube_cells = cube_cells.transpose(0, 1, 4, 2, 3)
    return cube_cells.reshape(leading + (edge_cells, edge_cells * edge_cells))


def restored(block_cells, direction):
    leading = block_cells.shape[:2]
    edge_cells = block_cells.shape[2]
    cube_cells = block_cells.reshape(leading + (edge_cells, edge_cells, edge_cells))
    if direction == 1:
        cube_cells = cube_cells.transpose(0, 1, 3, 2, 4)
    elif direction == 2:
        cube_cells = cube_cells.transpose(0, 1, 3, 4, 2)
    return cube_cells.reshape(leading + (edge_cells, edge_cells * edge_cells))


def advance(block_cells, ghosts):
    divergence = jnp.zeros_like(block_cells)
    boundary = []
    for direction in range(3):
        padded = jnp.concatenate(
            [ghosts[2 * direction], oriented(block_cells, direction), ghosts[2 * direction + 1]],
            axis=2,
        )
        fluxes = face_fluxes(padded, direction)
        divergence = divergence + restored(fluxes[:, :, 1:] - fluxes[:, :, :-1], direction)
        boundary.append(fluxes[:, :, 0])
        boundary.append(fluxes[:, :, -1])
    return (block_cells - STEP_RATIO * divergence, jnp.stack(boundary))


def face_slabs(block_cells, layers):
    edge_cells = block_cells.shape[2]
    pieces = []
    for direction in range(3):
        view_cells = oriented(block_cells, direction)
        pieces.append(view_cells[:, :, :layers])
        pieces.append(view_cells[:, :, edge_cells - layers :])
    return jnp.stack(pieces).transpose(2, 0, 1, 3, 4)


def inner_rim(ghost_slabs):
    return jnp.stack([ghost_slabs[:, face_id, :, 1 - face_id % 2] for face_id in range(6)], axis=1)


def flipped_octant(octants, mask_bit):
    return octants + mask_bit - 2 * mask_bit * (octants // mask_bit % 2)


def fine_ghosts(face_set, rims, octants, siblings):
    block_count = face_set.shape[0]
    edge_sq = face_set.shape[-1]
    half_edge = math.isqrt(edge_sq) // 2
    row_ids = jnp.arange(block_count)
    result = []
    for face_id in range(6):
        direction = face_id // 2
        side_id = face_id % 2
        outward = octants // BIT_OF[direction] % 2 == side_id
        first_bit = octants // TANGENT[direction][0] % 2
        second_bit = octants // TANGENT[direction][1] % 2
        coarse_rim = rims[:, face_id].reshape(block_count, 5, 2, half_edge, 2, half_edge)
        quarter = coarse_rim[row_ids, :, first_bit, :, second_bit, :]
        widened = jnp.repeat(jnp.repeat(quarter, 2, axis=2), 2, axis=3).reshape(
            block_count, 5, 1, edge_sq
        )
        from_coarse = jnp.concatenate([widened, widened], axis=2)
        from_sibling = face_set[siblings[:, direction], OPPOSITE[face_id]]
        result.append(jnp.where(outward[:, None, None, None], from_coarse, from_sibling))
    return jnp.stack(result).transpose(0, 2, 1, 3, 4)


def restricted(block_cells, flux_total, octants):
    block_count = block_cells.shape[1]
    half_edge = block_cells.shape[2] // 2
    averages = (
        block_cells.reshape(5, block_count, half_edge, 2, half_edge, 2, half_edge, 2).sum(
            axis=(3, 5, 7)
        )
        * 0.125
    )
    averages = averages.transpose(1, 0, 2, 3, 4)
    quarters = []
    for direction in range(3):
        outward_high = octants // BIT_OF[direction] % 2 == 1
        chosen = jnp.where(
            outward_high[None, :, None], flux_total[2 * direction + 1], flux_total[2 * direction]
        )
        summed = chosen.reshape(5, block_count, half_edge, 2, half_edge, 2).sum(axis=(3, 5))
        quarters.append(summed.transpose(1, 0, 2, 3) * 0.125)
    return (averages, jnp.stack(quarters, axis=1))


def assemble(averages, quarters, children, coarse_faces):
    block_count = children.shape[0]
    half_edge = averages.shape[-1]
    edge_cells = 2 * half_edge
    picked = averages[children].reshape(block_count, 2, 2, 2, 5, half_edge, half_edge, half_edge)
    new_cells = picked.transpose(4, 0, 1, 5, 2, 6, 3, 7).reshape(
        5, block_count, edge_cells, edge_cells * edge_cells
    )
    deltas = []
    for face_id in range(6):
        direction = face_id // 2
        side_id = face_id % 2
        octant_list = []
        for first_bit in (0, 1):
            for second_bit in (0, 1):
                octant_list.append(
                    side_id * BIT_OF[direction]
                    + first_bit * TANGENT[direction][0]
                    + second_bit * TANGENT[direction][1]
                )
        chosen = quarters[children[:, jnp.array(octant_list, jnp.int32)]][:, :, direction]
        fine_face = (
            chosen.reshape(block_count, 2, 2, 5, half_edge, half_edge)
            .transpose(0, 3, 1, 4, 2, 5)
            .reshape(block_count, 5, edge_cells * edge_cells)
        )
        deltas.append(coarse_faces[face_id].transpose(1, 0, 2) - fine_face)
    return (new_cells, jnp.stack(deltas, axis=1))


def apply_corrections(block_cells, corrections):
    edge_cells = block_cells.shape[2]
    for direction in range(3):
        view_cells = oriented(block_cells, direction)
        view_cells = view_cells.at[:, :, 0].add(corrections[:, 2 * direction].transpose(1, 0, 2))
        view_cells = view_cells.at[:, :, edge_cells - 1].add(
            corrections[:, 2 * direction + 1].transpose(1, 0, 2)
        )
        block_cells = restored(view_cells, direction)
    return block_cells


def local(fluid_state, neighbours, parents):
    level_id = lax.axis_index("level")
    blk_index = lax.axis_index("blk")
    device_count = lax.axis_size("blk")
    block_cells = fluid_state[0].transpose(1, 0, 2, 3)
    block_count = block_cells.shape[1]
    edge_cells = block_cells.shape[2]
    capacity = 2 * ((6 * block_count + device_count - 1) // device_count)
    own_rows = lax.dynamic_slice_in_dim(
        neighbours, blk_index * block_count, block_count, 0
    ).reshape(-1)
    item_ids = jnp.arange(6 * block_count, dtype=jnp.int32)
    targets = own_rows // block_count
    send_rank = jnp.sum(
        (targets[:, None] == targets[None, :]) & (item_ids[None, :] < item_ids[:, None]), axis=1
    )
    face_ids = item_ids % 6
    wanted = own_rows % block_count * 6 + face_ids + 1 - 2 * (face_ids % 2)
    their_rows = (
        neighbours.reshape(-1)[(targets * 6 * block_count)[:, None] + item_ids[None, :]]
        // block_count
    )
    recv_rank = jnp.sum((their_rows == blk_index) & (item_ids[None, :] < wanted[:, None]), axis=1)

    def spread(payload):
        return (
            jnp.zeros((device_count, capacity) + payload.shape[1:], payload.dtype)
            .at[targets, send_rank]
            .set(payload)
        )

    def collect(received):
        return received[targets, recv_rank]

    def route(buffer):
        return lax.all_to_all(buffer, "blk", split_axis=0, concat_axis=0, tiled=True)

    def trade_faces(cells_now):
        face_set = face_slabs(cells_now, 2)
        received = route(spread(face_set.reshape(6 * block_count, 5, 2, -1)))
        return (face_set, collect(received).reshape(block_count, 6, 5, 2, -1))

    parent_rows = lax.dynamic_slice_in_dim(parents, blk_index * block_count, block_count, 0)
    parent_local = parent_rows[:, 0] - blk_index * block_count
    octants = parent_rows[:, 1]
    parents_here = block_count // 8
    refined = jnp.zeros((block_count,), jnp.int32).at[parent_local].set(1)
    packed_slot = jnp.cumsum(refined) - 1
    target_slot = jnp.where(refined > 0, packed_slot, parents_here)
    rim_source = packed_slot[parent_local]
    children = (
        jnp.zeros((block_count, 8), jnp.int32)
        .at[parent_local, octants]
        .set(jnp.arange(block_count, dtype=jnp.int32))
    )
    siblings = jnp.stack(
        [
            children[parent_local, flipped_octant(octants, BIT_OF[direction])]
            for direction in range(3)
        ],
        axis=1,
    )

    def lend_rims(all_rims):
        packed = (
            jnp.zeros((parents_here,) + all_rims.shape[1:], all_rims.dtype)
            .at[target_slot]
            .set(all_rims, mode="drop")
        )
        lent_rims = shifted(packed, "level", 1)
        return lent_rims[rim_source]

    early_slabs, early_ghosts = trade_faces(block_cells)
    early_rims = lend_rims(inner_rim(early_ghosts))
    fine_early = fine_ghosts(early_slabs, early_rims, octants, siblings)
    first_ghosts = jnp.where(level_id == 0, early_ghosts.transpose(1, 2, 0, 3, 4), fine_early)
    cells_half, first_faces = advance(block_cells, first_ghosts)
    late_slabs, late_ghosts = trade_faces(cells_half)
    late_all = inner_rim(late_ghosts)
    late_rims = lend_rims(late_all)
    later_ghosts = fine_ghosts(late_slabs, 0.5 * (early_rims + late_rims), octants, siblings)
    cells_out, second_faces = lax.cond(
        level_id == 1,
        lambda: advance(cells_half, later_ghosts),
        lambda: (cells_half, jnp.zeros_like(first_faces)),
    )
    flux_total = first_faces + second_faces
    half_edge = edge_cells // 2
    averages, quarters = restricted(cells_out, flux_total, octants)
    bundle = jnp.concatenate(
        [averages.reshape(block_count, -1), quarters.reshape(block_count, -1)], axis=1
    )
    moved = shifted(bundle, "level", -1)
    split_at = 5 * half_edge**3
    averages = moved[:, :split_at].reshape(block_count, 5, half_edge, half_edge, half_edge)
    quarters = moved[:, split_at:].reshape(block_count, 3, 5, half_edge, half_edge)
    parent_cells, deltas = assemble(averages, quarters, children, first_faces)
    refined_mask = refined.astype(jnp.float32)
    coarse_mixed = jnp.where(refined_mask[None, :, None, None] > 0.0, parent_cells, cells_half)
    deltas = deltas * refined_mask[:, None, None, None]
    returned = collect(route(spread(deltas.reshape(6 * block_count, 5, -1))))
    corrections = (
        returned.reshape(block_count, 6, 5, -1)
        * jnp.array(FACE_SIGNS, jnp.float32)[None, :, None, None]
        * STEP_RATIO
    )
    coarse_out = apply_corrections(coarse_mixed, corrections)
    finished = jnp.where(level_id == 0, coarse_out, cells_out)
    return finished.transpose(1, 0, 2, 3)[None]


def solution(mesh):
    return jax.shard_map(
        local,
        mesh=mesh,
        in_specs=(P("level", "blk", None, None, None), P(), P()),
        out_specs=P("level", "blk", None, None, None),
        check_vma=False,
    )
```

profile of v0, /device:TPU:2, one launch (start us, length us, event | category | flops | bytes accessed | tf_op | source)
XLA Modules:
  0.0 915.3 jit_solution(11139200420147942258)
XLA Ops:
  2.3 2.1 copy.1754
  4.3 5.9 reshape.1808
  10.3 13.9 %copy.1753 = f32[5,16,16,16,16]{4,2,1,3,0:T(8,128)} copy(f32[5,16,16,16,16]{4,3,1,0,2:T(8,128)} %reshape.1808) | data formatting | bytes 2621440 | tf_op jit(solution)/shard_map/reshape | solution.py:104
  24.1 12.7 %copy.1442 = f32[5,16,16,16,16]{3,2,1,4,0:T(8,128)} copy(f32[5,16,16,16,16]{4,3,1,0,2:T(8,128)} %reshape.1808) | data formatting | bytes 2621440 | tf_op jit(solution)/shard_map/reshape | solution.py:104
  37.8 51.2 %gather_fusion = s32[9216]{0:T(1024)S(1)} fusion(s32[12288]{0:T(1024)S(1)} %reshape.1812, s32[9216]{0:T(1024)S(1)} %broadcast_clamp_fusion), kind=kCustom, calls=%fused_computation | custom fusion | bytes 110592 | tf_op jit(solution)/shard_map/gather | solution.py:261
  90.8 7.3 reshape.1809
  99.6 8.3 reshape.1810
  113.3 2.2 broadcast.2057.clone
  115.5 12.8 %scatter_fusion = f32[128,2,5,2,256]{4,3,2,1,0:T(2,128)} fusion(f32[128,2,5,2,256]{4,3,2,1,0:T(2,128)} %broadcast.2057.clone, s32[96]{0:T(128)S(1)} %fusion.321, f32[96,5,2,256]{3,2,1,0:T(2,128)S(1)} %bitcast.1399), kind=kCustom, calls=%fused_computation.48 | custom fusion | bytes 2949888 | tf_op jit(solution)/shard_map/scatter | solution.py:270
  128.3 15.8 %all-to-all-start = ((f32[128,2,5,2,256]{4,3,2,1,0:T(2,128)}), f32[128,2,5,2,256]{4,3,2,1,0:T(2,128)}, u32[]{:S(2)}, u32[]{:S(2)}) async-start(f32[128,2,5,2,256]{4,3,2,1,0:T(2,128)} %scatter_fusion), calls=%async_computation | async-start | bytes 5242880 | tf_op jit(solution)/shard_map/all_to_all | solution.py:277
  158.7 48.7 %all-to-all-done = f32[128,2,5,2,256]{4,3,2,1,0:T(2,128)} async-done(((f32[128,2,5,2,256]{4,3,2,1,0:T(2,128)}), f32[128,2,5,2,256]{4,3,2,1,0:T(2,128)}, u32[]{:S(2)}, u32[]{:S(2)}) %all-to-all-start) | async-done | bytes 2621472 | tf_op jit(solution)/shard_map/all_to_all | solution.py:277
  207.4 4.0 gather_fusion.1
  212.6 2.4 stack.143
  221.2 3.1 copy.1456
  228.6 2.0 copy.1466
  234.9 2.0 copy.1473
  241.2 2.0 copy.1483
  247.5 2.0 copy.1490
  282.9 7.2 reshape.1823
  290.1 12.3 %copy.1536 = f32[5,16,16,16,16]{4,3,1,0,2:T(8,128)} copy(f32[5,16,16,16,16]{3,2,1,4,0:T(8,128)} %bitcast.1384) | data formatting | bytes 2621440 | tf_op jit(solution)/shard_map/transpose | solution.py:119
  302.4 8.2 reshape.1824
  310.6 3.3 fusion.126
  322.7 7.4 reshape.1821
  330.1 11.3 %copy.1533 = f32[5,16,16,16,16]{4,3,1,0,2:T(8,128)} copy(f32[5,16,16,16,16]{4,2,3,1,0:T(8,128)} %bitcast.1385) | data formatting | bytes 2621440 | tf_op jit(solution)/shard_map/transpose | solution.py:117
  341.3 8.2 reshape.1822
  361.4 6.1 reshape.1825
  368.2 13.9 %copy.1537 = f32[5,16,16,16,16]{4,3,1,0,2:T(8,128)} copy(f32[5,16,16,16,16]{4,2,1,0,3:T(8,128)} %bitcast.1379) | data formatting | bytes 2621440 | tf_op jit(solution)/shard_map/transpose | solution.py:106
  382.1 7.3 reshape.1826
  391.5 12.7 %copy.1538 = f32[5,16,16,16,16]{4,3,1,0,2:T(8,128)} copy(f32[5,16,16,16,16]{2,4,1,0,3:T(8,128)} %bitcast.1380) | data formatting | bytes 2621440 | tf_op jit(solution)/shard_map/transpose | solution.py:108
  404.2 7.3 reshape.1827
  414.9 2.2 broadcast.2057
  417.1 12.8 %scatter_fusion.3 = f32[128,2,5,2,256]{4,3,2,1,0:T(2,128)} fusion(f32[128,2,5,2,256]{4,3,2,1,0:T(2,128)} %broadcast.2057, s32[96]{0:T(128)S(1)} %fusion.321, f32[96,5,2,256]{3,2,1,0:T(2,128)S(1)} %bitcast.1398), kind=kCustom, calls=%fused_computation.51 | custom fusion | bytes 2949888 | tf_op jit(solution)/shard_map/scatter | solution.py:270
  429.9 8.1 all-to-all-start.1
  450.4 50.7 %all-to-all-done.1 = f32[128,2,5,2,256]{4,3,2,1,0:T(2,128)} async-done(((f32[128,2,5,2,256]{4,3,2,1,0:T(2,128)}), f32[128,2,5,2,256]{4,3,2,1,0:T(2,128)}, u32[]{:S(2)}, u32[]{:S(2)}) %all-to-all-start.1) | async-done | bytes 2621472 | tf_op jit(solution)/shard_map/all_to_all | solution.py:277
  501.1 4.0 gather_fusion.19
  506.2 2.5 stack.170
  541.5 13.0 %conditional.1 = (f32[5,16,16,256]{3,2,1,0:T(8,128)}, f32[6,5,16,256]{3,2,1,0:T(8,128)}) conditional(s32[]{:T(128)} %convert_element_type.13, (f32[5,16,16,256]{3,1,0,2:T(8,128)S(1)}) %tuple.47, (f32[6,5,16,2,256]{4,2,3,1,0:T(8,128)S(1)}, f32[5,16,16,256]{3,1,0,2:T(8,128)S(1)}) %tuple.269), branch_computations={%region_21.22_spmd, %region_22.35_spmd} | conditional | flops 89956344 | bytes 339861696 | solution.py:323
  554.5 6.7 copy.1590
  561.2 10.5 %reduce_sum.290 = f32[5,16,8,8,8]{1,4,3,2,0:T(8,128)S(1)} reduce(f32[5,16,8,2,8,2,8,2]{1,7,6,5,4,3,2,0:T(2,128)} %bitcast.1393, f32[]{:T(128)} %constant.551.clone.1), dimensions={3,5,7}, to_apply=%region_35.36 | reduce | flops 286720 | bytes 1474564 | tf_op jit(solution)/shard_map/reduce_sum | solution.py:183
  580.5 139.0 %collective-permute-done.2 = f32[16,3520]{1,0:T(8,128)S(1)} collective-permute-done((f32[16,3520]{1,0:T(8,128)S(1)}, f32[16,3520]{1,0:T(8,128)S(1)}, u32[]{:S(2)}, u32[]{:S(2)}) %collective-permute-start.2) | collective-permute-done | bytes 225312 | tf_op jit(solution)/shard_map/ppermute | solution.py:19
  720.6 2.7 gather_fusion.35
  726.4 2.7 gather_fusion.37
  731.4 2.7 gather_fusion.39
  737.0 2.7 gather_fusion.41
  742.6 2.7 gather_fusion.43
  747.6 2.7 gather_fusion.45
  758.3 4.4 scatter_fusion.5
  764.4 23.3 %all-to-all-start.2 = ((f32[128,2,5,256]{3,1,2,0:T(2,128)}), f32[128,2,5,256]{3,1,2,0:T(2,128)}, u32[]{:S(2)}, u32[]{:S(2)}) async-start(f32[128,2,5,256]{3,1,2,0:T(2,128)} %copy.1639), calls=%async_computation.2 | async-start | bytes 2621440 | tf_op jit(solution)/shard_map/all_to_all | solution.py:277
  789.2 3.2 copy.1603
  792.4 8.9 gather_fusion.33
  801.3 16.7 %copy.1604 = f32[5,16,2,8,2,8,2,8]{1,7,6,5,4,3,2,0:T(8,128)} copy(f32[5,16,2,8,2,8,2,8]{7,5,3,0,6,4,2,1:T(8,128)} %bitcast.1381) | data formatting | bytes 2621440 | tf_op jit(solution)/shard_map/transpose | solution.py:205
  818.0 6.9 copy.1605
  826.5 3.0 copy.1640
  829.5 2.6 gather_fusion.46
  832.5 6.0 reshape_reshape_reshape.3
  838.5 13.9 %copy.1643 = f32[5,16,16,16,16]{4,3,1,0,2:T(8,128)} copy(f32[5,16,16,16,16]{4,2,1,0,3:T(8,128)} %bitcast.1389) | data formatting | bytes 2621440 | tf_op jit(solution)/shard_map/transpose | solution.py:106
  852.5 7.3 reshape.1852
  859.9 6.0 reshape.1855
  865.9 13.6 %copy.1644 = f32[5,16,16,16,16]{2,3,1,0,4:T(8,128)} copy(f32[5,16,16,16,16]{4,3,1,0,2:T(8,128)} %reshape.1855) | data formatting | bytes 2621440 | tf_op jit(solution)/shard_map/reshape | solution.py:115
  879.5 7.3 reshape.1856
  886.9 6.0 reshape.1859
  892.9 12.2 %copy.1645 = f32[5,16,16,16,16]{4,3,2,0,1:T(8,128)} copy(f32[5,16,16,16,16]{3,2,1,0,4:T(8,128)} %bitcast.1391) | data formatting | bytes 2621440 | tf_op jit(solution)/shard_map/transpose | solution.py:119
  905.1 7.3 reshape.1860
  912.5 2.6 fusion.147
  (598 shorter events, 194.4 us)
Async XLA Ops:
  0.0 144.1 %copy-start = (s32[2048,2]{0,1:T(2,128)S(1)}, s32[2048,2]{0,1:T(2,128)}, u32[]{:S(2)}) copy-start(s32[2048,2]{0,1:T(2,128)} %param.26) | copy-start | bytes 49156
  4.3 5.9 copy-start.17
  37.8 51.3 %copy-start.15 = (f32[1,16,5,16,256]{4,3,2,1,0:T(8,128)S(1)}, f32[1,16,5,16,256]{4,3,2,1,0:T(8,128)}, u32[]{:S(2)}) copy-start(f32[1,16,5,16,256]{4,3,2,1,0:T(8,128)} %param.24) | copy-start | bytes 3932164
  98.2 9.8 %copy-start.25 = (f32[5,16,16,256]{3,1,2,0:T(8,128)}, f32[5,16,16,256]{3,1,2,0:T(8,128)S(1)}, u32[]{:S(2)}) copy-start(f32[5,16,16,256]{3,1,2,0:T(8,128)S(1)} %reshape.1809) | copy-start | bytes 3932164
  113.3 387.8 %copy-start.4 = (s32[96]{0:T(128)}, s32[96]{0:T(128)S(1)}, u32[]{:S(2)}) copy-start(s32[96]{0:T(128)S(1)} %get-tuple-element.250) | copy-start | bytes 1156
  113.3 303.7 %copy-start.6 = (s32[96]{0:T(128)}, s32[96]{0:T(128)S(1)}, u32[]{:S(2)}) copy-start(s32[96]{0:T(128)S(1)} %fusion.321) | copy-start | bytes 1156
  128.3 79.1 %all-to-all-start = ((f32[128,2,5,2,256]{4,3,2,1,0:T(2,128)}), f32[128,2,5,2,256]{4,3,2,1,0:T(2,128)}, u32[]{:S(2)}, u32[]{:S(2)}) async-start(f32[128,2,5,2,256]{4,3,2,1,0:T(2,128)} %scatter_fusion), calls=%async_computation | async-start | bytes 5242880 | tf_op jit(solution)/shard_map/all_to_all | solution.py:277
  145.3 12.8 %copy-start.92 = (s32[16]{0:T(128)}, s32[16]{0:T(128)S(1)}, u32[]{:S(2)}) copy-start(s32[16]{0:T(128)S(1)} %scatter_custom_fusion) | copy-start | bytes 196
  151.6 59.9 %copy-start.51 = (s32[16]{0:T(128)}, s32[16]{0:T(128)S(1)}, u32[]{:S(2)}) copy-start(s32[16]{0:T(128)S(1)} %get-tuple-element.115) | copy-start | bytes 196
  155.2 57.4 %copy-start.53 = (s32[16]{0:T(128)}, s32[16]{0:T(128)S(1)}, u32[]{:S(2)}) copy-start(s32[16]{0:T(128)S(1)} %get-tuple-element.108) | copy-start | bytes 196
  155.2 57.4 %copy-start.55 = (s32[16]{0:T(128)}, s32[16]{0:T(128)S(1)}, u32[]{:S(2)}) copy-start(s32[16]{0:T(128)S(1)} %get-tuple-element.109) | copy-start | bytes 196
  158.6 56.4 %copy-start.89 = (s32[16]{0:T(128)}, s32[16]{0:T(128)S(1)}, u32[]{:S(2)}) copy-start(s32[16]{0:T(128)S(1)} %get-tuple-element.422) | copy-start | bytes 196
  158.6 105.7 %copy-start.81 = (pred[16]{0:T(512)(128)(4,1)}, pred[16]{0:T(512)(128)(4,1)S(1)}, u32[]{:S(2)}) copy-start(pred[16]{0:T(512)(128)(4,1)S(1)} %get-tuple-element.244) | copy-start | bytes 52
  158.7 101.4 %copy-start.76 = (pred[16]{0:T(512)(128)(4,1)}, pred[16]{0:T(512)(128)(4,1)S(1)}, u32[]{:S(2)}) copy-start(pred[16]{0:T(512)(128)(4,1)S(1)} %get-tuple-element.417) | copy-start | bytes 52
  158.7 103.5 %copy-start.74 = (pred[16]{0:T(512)(128)(4,1)}, pred[16]{0:T(512)(128)(4,1)S(1)}, u32[]{:S(2)}) copy-start(pred[16]{0:T(512)(128)(4,1)S(1)} %get-tuple-element.246) | copy-start | bytes 52
  158.7 104.6 %copy-start.83 = (pred[16]{0:T(512)(128)(4,1)}, pred[16]{0:T(512)(128)(4,1)S(1)}, u32[]{:S(2)}) copy-start(pred[16]{0:T(512)(128)(4,1)S(1)} %get-tuple-element.423) | copy-start | bytes 52
  158.7 100.2 %copy-start.87 = (pred[16]{0:T(512)(128)(4,1)}, pred[16]{0:T(512)(128)(4,1)S(1)}, u32[]{:S(2)}) copy-start(pred[16]{0:T(512)(128)(4,1)S(1)} %get-tuple-element.431) | copy-start | bytes 52
  158.7 102.4 %copy-start.85 = (pred[16]{0:T(512)(128)(4,1)}, pred[16]{0:T(512)(128)(4,1)S(1)}, u32[]{:S(2)}) copy-start(pred[16]{0:T(512)(128)(4,1)S(1)} %get-tuple-element.432) | copy-start | bytes 52
  216.2 2.2 collective-permute-start
  217.7 3.5 copy-start.80
  219.0 5.3 copy-start.27
  257.9 4.3 copy-start.42
  259.0 4.3 copy-start.44
  259.0 5.4 copy-start.43
  259.0 5.4 copy-start.63
  271.0 2.9 copy-start.13
  271.1 2.9 copy-start.32
  302.4 8.2 copy-start.41
  349.5 2.8 copy-start.9
  349.5 2.8 copy-start.14
  349.5 2.8 copy-start.35
  349.5 2.8 copy-start.36
  357.8 2.5 copy-start.16
  357.8 2.5 copy-start.29
  357.8 2.5 copy-start.30
  361.3 180.2 %copy-start.2 = (f32[5,16,16,256]{3,1,0,2:T(8,128)}, f32[5,16,16,256]{3,1,0,2:T(8,128)S(1)}, u32[]{:S(2)}) copy-start(f32[5,16,16,256]{3,1,0,2:T(8,128)S(1)} %fusion.146) | copy-start | bytes 3932164
  429.8 8.7 copy-start.99
  429.8 9.6 %copy-start.98 = (s32[4]{0:T(128)S(1)}, s32[4]{0:T(128)}, u32[]{:S(2)}) copy-start(s32[4]{0:T(128)} %constant.1156) | copy-start | bytes 52
  429.9 10.2 %copy-start.97 = (s32[4]{0:T(128)S(1)}, s32[4]{0:T(128)}, u32[]{:S(2)}) copy-start(s32[4]{0:T(128)} %constant.1157) | copy-start | bytes 52
  429.9 12.3 %copy-start.96 = (s32[4]{0:T(128)S(1)}, s32[4]{0:T(128)}, u32[]{:S(2)}) copy-start(s32[4]{0:T(128)} %constant.1158) | copy-start | bytes 52
  429.9 71.2 %all-to-all-start.1 = ((f32[128,2,5,2,256]{4,3,2,1,0:T(2,128)}), f32[128,2,5,2,256]{4,3,2,1,0:T(2,128)}, u32[]{:S(2)}, u32[]{:S(2)}) async-start(f32[128,2,5,2,256]{4,3,2,1,0:T(2,128)} %scatter_fusion.3), calls=%async_computation.1 | async-start | bytes 5242880 | tf_op jit(solution)/shard_map/all_to_all | solution.py:277
  505.1 3.6 copy-start.90
  508.7 7.0 copy-start.52
  508.7 9.8 %copy-start.56 = (s32[16]{0:T(128)S(1)}, s32[16]{0:T(128)}, u32[]{:S(2)}) copy-start(s32[16]{0:T(128)} %copy-done.55) | copy-start | bytes 196
  509.9 10.0 %copy-start.54 = (s32[16]{0:T(128)S(1)}, s32[16]{0:T(128)}, u32[]{:S(2)}) copy-start(s32[16]{0:T(128)} %copy-done.53) | copy-start | bytes 196
  509.9 10.8 %collective-permute-start.1 = (f32[2,6,5,256]{3,1,2,0:T(8,128)S(1)}, f32[2,6,5,256]{3,1,2,0:T(8,128)S(1)}, u32[]{:S(2)}, u32[]{:S(2)}) collective-permute-start(f32[2,6,5,256]{3,1,2,0:T(8,128)S(1)} %scatter_fusion.4), channel_id=1, source_target_pairs={{0,128},{1,129},{2,130},{3,131},{4,132},{5,133},{6,134},{7,135},{8... | collective-permute-start | bytes 184328 | tf_op jit(solution)/shard_map/ppermute | solution.py:19
  515.8 5.7 copy-start.28
  578.0 1.9 copy-start.91
  578.0 1.9 copy-start.79
  578.0 2.1 copy-start.78
  578.0 2.3 copy-start.94
  578.3 142.3 %copy-start.72 = (s32[1024]{0:T(1024)S(1)}, s32[1024]{0:T(1024)}, u32[]{:S(2)}) copy-start(s32[1024]{0:T(1024)} %pad_clamp_fusion.10) | copy-start | bytes 12292
  578.3 141.2 %collective-permute-start.2 = (f32[16,3520]{1,0:T(8,128)S(1)}, f32[16,3520]{1,0:T(8,128)S(1)}, u32[]{:S(2)}, u32[]{:S(2)}) collective-permute-start(f32[16,3520]{1,0:T(8,128)S(1)} %pad_maximum_fusion.13), channel_id=1, source_target_pairs={{128,0},{129,1},{130,2},{131,3},{132,4},{133,5},{134,6},{135,7},{1... | collective-permute-start | bytes 675848 | tf_op jit(solution)/shard_map/ppermute | solution.py:19
  724.7 1.8 copy-start.71
  751.7 1.8 copy-start.61
  751.7 2.7 copy-start.62
  764.4 23.3 %copy-start.93 = (s32[16]{0:T(128)S(1)}, s32[16]{0:T(128)}, u32[]{:S(2)}) copy-start(s32[16]{0:T(128)} %copy-done.92) | copy-start | bytes 196
  764.4 23.3 %slice-start = ((f32[16,3520]{1,0:T(8,128)}), f32[16,2560]{1,0:T(8,128)S(1)}, s32[]{:S(2)}) async-start(f32[16,3520]{1,0:T(8,128)} %copy-done.50), calls=%async_computation.3 | async-start | bytes 327680 | tf_op jit(solution)/shard_map/slice | solution.py:336
  764.4 62.1 %all-to-all-start.2 = ((f32[128,2,5,256]{3,1,2,0:T(2,128)}), f32[128,2,5,256]{3,1,2,0:T(2,128)}, u32[]{:S(2)}, u32[]{:S(2)}) async-start(f32[128,2,5,256]{3,1,2,0:T(2,128)} %copy.1639), calls=%async_computation.2 | async-start | bytes 2621440 | tf_op jit(solution)/shard_map/all_to_all | solution.py:277
  789.2 3.2 copy-start.73
  818.0 6.9 copy-start.3
  826.5 3.0 copy-start.5
  829.5 2.6 copy-start.95
  905.1 10.0 %copy-start.1 = (s32[2048,2]{0,1:T(2,128)S(1)}, s32[2048,2]{0,1:T(2,128)}, u32[]{:S(2)}) copy-start(s32[2048,2]{0,1:T(2,128)} %param.26) | copy-start | bytes 49156
  (37 other events, 40.6 us)
where the time goes:
time: 932 us; the launch traced here: 915 us
  local copies, waits for them, and re-layouts  543 us (58%)
  waiting for transfers between devices  239 us (26%)
  other arithmetic  68.3 us (7%)
  starting transfers between devices  51.8 us (6%)
  loops' own time  10.3 us (1%)
    ppermute x3, waiting for transfers between devices, shifted(): return lax.ppermute(array, axis, pairs)  140 us
    all_to_all x3, waiting for transfers between devices, route(): lax.all_to_all(buffer, 'blk', split_axis=0, concat_axis=0, tiled=True)  99.4 us
    gather x2, local copies, waits for them, and re-layouts, local(): neighbours.reshape(-1)  51.2 us
    all_to_all x3, starting transfers between devices, route(): lax.all_to_all(buffer, 'blk', split_axis=0, concat_axis=0, tiled=True)  47.1 us
    reshape x6, local copies, waits for them, and re-layouts, oriented(): return cube_cells.reshape(leading + (edge_cells, edge_cells * edge_cells))  45 us
    reshape x5, local copies, waits for them, and re-layouts, restored(): block_cells.reshape(leading + (edge_cells, edge_cells, edge_cells))  40.2 us
    reshape x4, local copies, waits for them, and re-layouts, oriented(): block_cells.reshape(leading + (edge_cells, edge_cells, edge_cells))  38.7 us
    scatter x4, local copies, waits for them, and re-layouts, spread(): return jnp.zeros((device_count, capacity) + payload.shape[1:], payload.dt...  31.7 us
  transfers between devices with their start and end apart: 6, of which 4 were waited for; matrix products, arithmetic and copies ran while one was open for 8% of the time, Pallas kernels for 0%

commit v1 on v0

v1 whole, which is shorter than its diff:
```python
import jax
import jax.numpy as jnp
from jax import lax
from jax.experimental import pallas as pl
from jax.experimental.pallas import tpu as pltpu
from jax.sharding import PartitionSpec as P

GAMMA = 1.4
RATIO = 0.12
MESH = pl.DeviceIdType.MESH
ORDER = ((0, 1, 2, 3, 4), (0, 2, 1, 3, 4), (0, 3, 1, 2, 4))
BIT_OF = (4, 2, 1)
TANGENT = ((2, 1), (4, 1), (4, 2))
F32 = jnp.float32


def iota(axis):
    return lax.broadcasted_iota(jnp.int32, (8, 128), axis)


def take(tile, index):
    return jnp.take_along_axis(tile, index, axis=1, mode="promise_in_bounds")


def flip8(tiles):
    return jnp.swapaxes(jnp.stack(tiles), 0, 1)


def swap_groups(tiles):
    tiles = list(tiles)
    lane = iota(1)
    for step in (1, 2, 4):
        upper = (lane // 16) % (2 * step) >= step
        for i in range(8):
            if i & step == 0:
                a, b = tiles[i], tiles[i + step]
                tiles[i] = jnp.where(upper, pltpu.roll(b, 16 * step, 1), a)
                tiles[i + step] = jnp.where(upper, b, pltpu.roll(a, 128 - 16 * step, 1))
    return tiles


def swap_lanes(low, high, part):
    lane = iota(1)
    index = (lane % 8) * 16 + 8 * part + lane // 16
    return jnp.where(lane % 16 < 8, take(low, index), take(high, index))


def prim(q):
    inverse = 1.0 / q[0]
    speed = q[1] * inverse
    kinetic = (q[1] * q[1] + q[2] * q[2] + q[3] * q[3]) * inverse
    return inverse, speed, (GAMMA - 1.0) * (q[4] - 0.5 * kinetic)


def flux_of(q, speed, pressure):
    return [q[1], q[1] * speed + pressure, q[2] * speed, q[3] * speed, (q[4] + pressure) * speed]


def half_step(below, here, above, low_wanted=True, high_wanted=True):
    low, high = [], []
    for u0, u1, u2 in zip(below, here, above):
        a = u1 - u0
        b = u2 - u1
        slope = jnp.maximum(jnp.minimum(a, b), 0.0) + jnp.minimum(jnp.maximum(a, b), 0.0)
        low.append(u1 - 0.5 * slope)
        high.append(u1 + 0.5 * slope)
    _, speed, pressure = prim(low)
    flux_low = flux_of(low, speed, pressure)
    _, speed, pressure = prim(high)
    flux_high = flux_of(high, speed, pressure)
    change = [0.5 * RATIO * (a - b) for a, b in zip(flux_low, flux_high)]
    low = [a + b for a, b in zip(low, change)] if low_wanted else None
    high = [a + b for a, b in zip(high, change)] if high_wanted else None
    return low, high


def with_sound(q):
    inverse, speed, pressure = prim(q)
    return q, inverse, speed, pressure, jnp.sqrt(GAMMA * pressure * inverse)


def contact_flux(low, high):
    ql, il, ul, pl_, cl = with_sound(low)
    qh, ih, uh, ph, ch = with_sound(high)
    slowest = jnp.minimum(ul - cl, uh - ch)
    fastest = jnp.maximum(ul + cl, uh + ch)
    mass_l = ql[0] * (slowest - ul)
    mass_h = qh[0] * (fastest - uh)
    contact = (ph - pl_ + ul * mass_l - uh * mass_h) / (mass_l - mass_h)
    lower = jnp.logical_or(slowest >= 0.0, contact >= 0.0)
    q = [jnp.where(lower, a, b) for a, b in zip(ql, qh)]
    inverse = jnp.where(lower, il, ih)
    speed = jnp.where(lower, ul, uh)
    pressure = jnp.where(lower, pl_, ph)
    mass = jnp.where(lower, mass_l, mass_h)
    wave = jnp.where(lower, slowest, fastest)
    outside = jnp.logical_or(slowest >= 0.0, jnp.logical_and(contact < 0.0, fastest <= 0.0))
    flux = flux_of(q, speed, pressure)
    over = 1.0 / (wave - contact)
    factor = mass * over
    scaled = factor * inverse
    gap = contact - speed
    star = [
        factor,
        factor * contact,
        scaled * q[2],
        scaled * q[3],
        scaled * q[4] + gap * (factor * contact + pressure * over),
    ]
    return [jnp.where(outside, f, f + wave * (s - u)) for f, s, u in zip(flux, star, q)]


def cells(V, a, i, ch):
    return [V[a, c, i, ch] for c in range(5)]


def ghost(G, a, s, layer, ch):
    return [G[2 * a + s, c, layer, ch] for c in range(5)]


def inner_sweep(V, D):
    def body(n, carry):
        a = n // 4
        ch = n % 4
        states = [cells(V, a, i, ch) for i in range(3)]
        _, high = half_step(*states)
        previous = None
        for i in range(2, 15):
            states = [states[1], states[2], cells(V, a, i + 1, ch)]
            low, next_high = half_step(*states)
            flux = contact_flux(high, low)
            for c in range(5):
                D[a, c, i - 1, ch] = flux[c] if previous is None else flux[c] - previous[c]
            high, previous = next_high, flux
        for c in range(5):
            D[a, c, 14, ch] = -previous[c]
        return carry

    lax.fori_loop(0, 12, body, 0)


def outer_sweep(V, G, D, FC, first):
    def body(n, carry):
        a = n // 4
        ch = n % 4
        u = [cells(V, a, i, ch) for i in range(3)]
        g = [ghost(G, a, 0, layer, ch) for layer in range(2)]
        _, r_ghost = half_step(g[0], g[1], u[0], low_wanted=False)
        l0, r0 = half_step(g[1], u[0], u[1])
        l1, _ = half_step(u[0], u[1], u[2], high_wanted=False)
        f0 = contact_flux(r_ghost, l0)
        f1 = contact_flux(r0, l1)
        for c in range(5):
            D[a, c, 0, ch] = f1[c] - f0[c]
            D[a, c, 1, ch] = D[a, c, 1, ch] - f1[c]
            FC[2 * a, c, ch] = f0[c] if first else FC[2 * a, c, ch] + f0[c]
        u = [cells(V, a, i, ch) for i in (13, 14, 15)]
        g = [ghost(G, a, 1, layer, ch) for layer in range(2)]
        _, r0 = half_step(u[0], u[1], u[2], low_wanted=False)
        l1, r1 = half_step(u[1], u[2], g[0])
        l2, _ = half_step(u[2], g[0], g[1], high_wanted=False)
        f0 = contact_flux(r0, l1)
        f1 = contact_flux(r1, l2)
        for c in range(5):
            D[a, c, 14, ch] = D[a, c, 14, ch] + f0[c]
            D[a, c, 15, ch] = f1[c] - f0[c]
            FC[2 * a + 1, c, ch] = f1[c] if first else FC[2 * a + 1, c, ch] + f1[c]
        return carry

    lax.fori_loop(0, 12, body, 0)


def update(V, D):
    def body(n, carry):
        t = n % 2
        X = n // 2
        for c in range(5):
            ys = [
                swap_groups([D[1, ORDER[1].index(c), 8 * Y + j, 2 * X + t] for j in range(8)])
                for Y in range(2)
            ]
            zs = [
                swap_groups([D[2, ORDER[2].index(c), 8 * Z + j, 2 * X + t] for j in range(8)])
                for Z in range(2)
            ]
            for i in range(8):
                for Y in range(2):
                    total = D[0, c, 8 * X + i, 2 * Y + t] + ys[Y][i]
                    total = total + swap_lanes(zs[0][i], zs[1][i], Y)
                    V[0, c, 8 * X + i, 2 * Y + t] = V[0, c, 8 * X + i, 2 * Y + t] - RATIO * total
        return carry

    lax.fori_loop(0, 4, body, 0)


def make_views(V):
    def body(n, carry):
        t = n % 2
        X = n // 2
        for c in range(5):
            for Y in range(2):
                tiles = swap_groups([V[0, c, 8 * X + i, 2 * Y + t] for i in range(8)])
                for j in range(8):
                    V[1, ORDER[1].index(c), 8 * Y + j, 2 * X + t] = tiles[j]
            for Z in range(2):
                tiles = swap_groups(
                    [
                        swap_lanes(V[0, c, 8 * X + i, t], V[0, c, 8 * X + i, 2 + t], Z)
                        for i in range(8)
                    ]
                )
                for j in range(8):
                    V[2, ORDER[2].index(c), 8 * Z + j, 2 * X + t] = tiles[j]
        return carry

    lax.fori_loop(0, 4, body, 0)


def load_state(fluid, perm, V):
    def body(c, carry):
        for t in range(2):
            for X in range(2):
                for h in range(2):
                    rows = flip8(
                        [
                            fluid[0, perm[8 * t + j], c, 8 * X : 8 * X + 8, 128 * h : 128 * h + 128]
                            for j in range(8)
                        ]
                    )
                    for i in range(8):
                        V[0, c, 8 * X + i, 2 * h + t] = rows[i]
        return carry

    lax.fori_loop(0, 5, body, 0)


def store_state(V, out):
    def body(c, carry):
        for t in range(2):
            for X in range(2):
                for h in range(2):
                    rows = flip8([V[0, c, 8 * X + i, 2 * h + t] for i in range(8)])
                    for j in range(8):
                        out[8 * t + j, c, 8 * X : 8 * X + 8, 128 * h : 128 * h + 128] = rows[j]
        return carry

    lax.fori_loop(0, 5, body, 0)


def make_slabs(V, items):
    def body(n, carry):
        f = n // 2
        t = n % 2
        a = f // 2
        first = (f % 2) * 14
        for c in range(5):
            four = [V[a, c, first + layer, 2 * h + t] for layer in range(2) for h in range(2)]
            rows = flip8(four + four)
            for j in range(8):
                items[f * 16 + 8 * t + j, c] = rows[j]
        return carry

    lax.fori_loop(0, 12, body, 0)


def make_rims(V, items):
    def body(n, carry):
        f = n // 2
        t = n % 2
        a = f // 2
        layer = (f % 2) * 15
        for c in range(5):
            two = [V[a, c, layer, 2 * h + t] for h in range(2)]
            rows = flip8(two * 4)
            for j in range(8):
                items[f * 16 + 8 * t + j, c] = rows[j, 0:4]
        return carry

    lax.fori_loop(0, 12, body, 0)


def pack(items, slots, send, rows):
    first = lax.broadcasted_iota(jnp.int32, (rows, 128), 0) < rows // 2

    def body(d, carry):
        i0 = slots[2 * d]
        i1 = slots[2 * d + 1]
        for c in range(5):
            send[d, c] = jnp.where(first, items[i0, c], items[i1, c])
        return carry

    lax.fori_loop(0, send.shape[0], body, 0)


def collect_slabs(recv, where, slot_mask, G):
    def body(n, carry):
        f = n // 2
        t = n % 2
        second = slot_mask[n] > 0.5
        for c in range(5):
            rows = flip8([recv[where[f * 16 + 8 * t + j], c] for j in range(8)])
            for layer in range(2):
                for h in range(2):
                    r = 2 * layer + h
                    G[f, c, layer, 2 * h + t] = jnp.where(second, rows[4 + r], rows[r])
        return carry

    lax.fori_loop(0, 12, body, 0)


def fine_ghosts(V, rims, G, late=None):
    lane = iota(1)
    sub = iota(0)
    for f in range(6):
        a, s = f // 2, f % 2
        bit = BIT_OF[a]
        outer = (sub // bit) % 2 == s
        first = (sub // TANGENT[a][0]) % 2 == 1
        second = (sub // TANGENT[a][1]) % 2

        def body(n, carry):
            t = n % 2
            c = n // 2

            def row(h):
                value = rims[f, c, pl.ds(2 * t + h, 1), :]
                if late is not None:
                    value = 0.5 * (value + late[f, c, pl.ds(2 * t + h, 1), :])
                return jnp.broadcast_to(value, (8, 128))

            source = jnp.where(first, row(1), row(0))
            for h in range(2):
                index = (4 * h + lane // 32) * 16 + 8 * second + (lane % 16) // 2
                coarse = take(source, index)
                for layer in range(2):
                    near = V[a, c, (layer if s else 14 + layer), 2 * h + t]
                    near = pltpu.roll(near, (8 - bit) if s else bit, 0)
                    G[f, c, layer, 2 * h + t] = jnp.where(outer, coarse, near)
            return carry

        lax.fori_loop(0, 10, body, 0)


def pair_sums(low, high, bit):
    lane = iota(1)
    index = (lane // 16 % 4) * 32 + 2 * (lane % 8)
    sums = []
    for tile in (low, high):
        tile = tile + pltpu.roll(tile, 127, 1)
        sums.append(take(tile + pltpu.roll(tile, 112, 1), index))
    merged = jnp.where(lane < 64, sums[0], sums[1])
    return jnp.where(lane % 16 < 8, merged, pltpu.roll(merged, 8 - bit, 0))


def restrict(V, FC, mixed, means):
    def body(n, carry):
        t = n % 2
        c = n // 2
        merged = []
        for x in range(8):
            low, high = [
                V[0, c, 2 * x, 2 * h + t] + V[0, c, 2 * x + 1, 2 * h + t] for h in range(2)
            ]
            merged.append(pair_sums(low, high, 1) * 0.125)
        rows = flip8(merged)
        for X in range(2):
            for h in range(2):
                mixed[t, c, X, h] = rows[4 * X + 2 * h]
        return carry

    lax.fori_loop(0, 10, body, 0)

    for f in range(6):
        a, s = f // 2, f % 2

        def face_body(c, carry):
            for t in range(2):
                merged = pair_sums(FC[f, c, t], FC[f, c, 2 + t], TANGENT[a][1]) * 0.125
                for h in range(2):
                    o = s * BIT_OF[a] + h * TANGENT[a][0]
                    means[f, c, 2 * t + h : 2 * t + h + 1, :] = merged[o : o + 1]
            return carry

        lax.fori_loop(0, 5, face_body, 0)


def take_mixed(V, mixed):
    top = iota(0) == 0

    def body(n, carry):
        t = n % 2
        c = n // 2
        for x in range(16):
            for h in range(2):
                row = jnp.broadcast_to(mixed[t, c, x // 8, h, x % 8 : x % 8 + 1, :], (8, 128))
                V[0, c, x, 2 * h + t] = jnp.where(top, row, V[0, c, x, 2 * h + t])
        return carry

    lax.fori_loop(0, 10, body, 0)


def apply_corrections(recv, where, slot_mask, V):
    lane = iota(1)

    for f in range(6):
        a, s = f // 2, f % 2
        scale = RATIO if s else -RATIO

        def body(t, carry):
            second = slot_mask[2 * f + t] > 0.5
            for k in range(5):
                c = ORDER[a][k]
                tiles = [recv[where[f * 16 + 8 * t + j], k] for j in range(8)]
                rows = flip8([jnp.concatenate([tile, tile], axis=0) for tile in tiles])
                change = [scale * jnp.where(second, rows[2 + h], rows[h]) for h in range(2)]
                if a == 0:
                    for h in range(2):
                        V[0, c, 15 * s, 2 * h + t] = V[0, c, 15 * s, 2 * h + t] + change[h]
                    continue
                for x in range(16):
                    source = change[x // 8]
                    i = x % 8
                    if a == 1:
                        group = 7 * s
                        moved = pltpu.roll(source, (16 * (group - i)) % 128, 1)
                        moved = jnp.where(lane // 16 == group, moved, 0.0)
                        V[0, c, x, 2 * s + t] = V[0, c, x, 2 * s + t] + moved
                    else:
                        for h in range(2):
                            moved = take(source, i * 16 + 8 * h + lane // 16)
                            moved = jnp.where(lane % 16 == 15 * s, moved, 0.0)
                            V[0, c, x, 2 * h + t] = V[0, c, x, 2 * h + t] + moved
            return carry

        lax.fori_loop(0, 2, body, 0)


def step_kernel(
    devices,
    perm,
    slots,
    where,
    which,
    fluid,
    slot_mask,
    out,
    V,
    D,
    G,
    FC,
    items1,
    items2,
    items3,
    send1,
    recv1,
    send2,
    recv2,
    send3,
    recv3,
    early_out,
    early_in,
    late_out,
    late_in,
    mixed_out,
    mixed_in,
    means_out,
    means_in,
    send_sems,
    recv_sems,
    pair_send,
    pair_recv,
):
    level = lax.axis_index("level")
    me = lax.axis_index("blk")
    other = 1 - level
    barrier = pltpu.get_barrier_semaphore()

    def start_all(send, recv, n):
        def body(d, carry):
            pltpu.make_async_remote_copy(
                src_ref=send.at[d],
                dst_ref=recv.at[d],
                send_sem=send_sems.at[n],
                recv_sem=recv_sems.at[n],
                device_id=(level, lax.rem(me + d + 1, devices)),
                device_id_type=MESH,
            ).start()
            return carry

        lax.fori_loop(0, devices - 1, body, 0)

    def whole(send, recv, n):
        return pltpu.make_async_remote_copy(
            src_ref=send,
            dst_ref=recv,
            send_sem=send_sems.at[n],
            recv_sem=recv_sems.at[n],
            device_id=(level, lax.rem(me + 1, devices)),
            device_id_type=MESH,
        )

    def to_pair(source, target, n):
        return pltpu.make_async_remote_copy(
            src_ref=source,
            dst_ref=target,
            send_sem=pair_send.at[n],
            recv_sem=pair_recv.at[n],
            device_id=(other, me),
            device_id_type=MESH,
        )

    pl.semaphore_signal(barrier, inc=1, device_id=(other, me), device_id_type=MESH)

    @pl.when(level == 0)
    def _():
        def greet(d, carry):
            pl.semaphore_signal(
                barrier,
                inc=1,
                device_id=(level, lax.rem(me + d + 1, devices)),
                device_id_type=MESH,
            )
            return carry

        lax.fori_loop(0, devices - 1, greet, 0)
        pl.semaphore_wait(barrier, devices)

    @pl.when(level == 1)
    def _():
        pl.semaphore_wait(barrier, 1)

    load_state(fluid, perm, V)
    make_views(V)

    @pl.when(level == 0)
    def _():
        make_slabs(V, items1)
        pack(items1, slots, send1, 8)
        start_all(send1, recv1, 0)

        def clear(n, carry):
            for c in range(5):
                items3[n, c] = jnp.zeros((4, 128), F32)
            return carry

        lax.fori_loop(0, 96, clear, 0)

    inner_sweep(V, D)

    @pl.when(level == 0)
    def _():
        whole(send1, recv1, 0).wait_recv()
        collect_slabs(recv1, where, slot_mask, G)
        for f in range(6):
            for c in range(5):
                for t in range(2):
                    for h in range(2):
                        early_out[f, c, 2 * t + h : 2 * t + h + 1, :] = G[
                            f, c, 1 - f % 2, 2 * h + t, 0:1, :
                        ]
        to_pair(early_out, early_in, 0).start()

    @pl.when(level == 1)
    def _():
        to_pair(early_out, early_in, 0).wait_recv()
        fine_ghosts(V, early_in, G)

    outer_sweep(V, G, D, FC, True)
    update(V, D)
    make_views(V)

    @pl.when(level == 0)
    def _():
        make_rims(V, items2)
        pack(items2, slots, send2, 4)
        start_all(send2, recv2, 1)
        whole(send2, recv2, 1).wait_recv()
        for f in range(6):
            for t in range(2):
                item = f * 16 + 8 * t
                for c in range(5):
                    tile = recv2[where[item], c]
                    late_out[f, c, 2 * t : 2 * t + 2, :] = jnp.where(
                        which[item] == 1, tile[2:4], tile[0:2]
                    )
        to_pair(late_out, late_in, 1).start()

        to_pair(mixed_out, mixed_in, 2).wait_recv()
        to_pair(means_out, means_in, 3).wait_recv()
        for f in range(6):
            for t in range(2):
                for c in range(5):
                    for h in range(2):
                        delta = (
                            FC[f, c, 2 * h + t, 0:1, :]
                            - means_in[f, c, 2 * t + h : 2 * t + h + 1, :]
                        )
                        for k in range(2):
                            items3[f * 16 + 8 * t, c, 2 * k + h : 2 * k + h + 1, :] = delta
        pack(items3, slots, send3, 4)
        start_all(send3, recv3, 2)
        take_mixed(V, mixed_in)
        whole(send3, recv3, 2).wait_recv()
        apply_corrections(recv3, where, slot_mask, V)

    @pl.when(level == 1)
    def _():
        inner_sweep(V, D)
        to_pair(late_out, late_in, 1).wait_recv()
        fine_ghosts(V, early_in, G, late_in)
        outer_sweep(V, G, D, FC, False)
        update(V, D)
        restrict(V, FC, mixed_out, means_out)
        to_pair(mixed_out, mixed_in, 2).start()
        to_pair(means_out, means_in, 3).start()

    store_state(V, out)

    @pl.when(level == 0)
    def _():
        whole(send1, recv1, 0).wait_send()
        whole(send2, recv2, 1).wait_send()
        whole(send3, recv3, 2).wait_send()
        to_pair(early_out, early_in, 0).wait_send()
        to_pair(late_out, late_in, 1).wait_send()

    @pl.when(level == 1)
    def _():
        to_pair(mixed_out, mixed_in, 2).wait_send()
        to_pair(means_out, means_in, 3).wait_send()


def place_kernel(back, source, out):
    def body(b, carry):
        out[0, b] = source[back[b]]
        return carry

    lax.fori_loop(0, out.shape[1], body, 0)


def tables(neighbours, parents, level, me, count, devices):
    rows = lax.dynamic_slice_in_dim(neighbours, me * count, count, 0)
    family = lax.dynamic_slice_in_dim(parents, me * count, count, 0)
    ids = jnp.arange(count, dtype=jnp.int32)
    owner = family[:, 0] - me * count
    owns = owner[:, None] == ids[None, :]
    is_parent = jnp.any(owns, axis=0)
    earlier = ids[None, :] < ids[:, None]
    parent_rank = jnp.sum(is_parent[None, :] & earlier, axis=1, dtype=jnp.int32)
    rest_rank = ids - parent_rank
    coarse_place = jnp.where(
        is_parent, 8 * parent_rank, jnp.where(rest_rank < 7, 1 + rest_rank, 2 + rest_rank)
    )
    fine_place = 8 * jnp.sum(jnp.where(owns, parent_rank[None, :], 0), axis=1) + family[:, 1]
    place = jnp.where(level == 0, coarse_place, fine_place).astype(jnp.int32)

    def inverse(position):
        return jnp.sum(
            jnp.where(position[None, :] == ids[:, None], ids[None, :], 0), axis=1, dtype=jnp.int32
        )

    coarse_perm = inverse(coarse_place)
    chosen = coarse_perm[:, None] == ids[None, :]
    ordered = jnp.sum(jnp.where(chosen[:, :, None], rows[None], 0), axis=1, dtype=jnp.int32)
    ordered = ordered.T.reshape(-1)
    faces = jnp.repeat(jnp.arange(6, dtype=jnp.int32), count)
    target = ordered // count
    own_id = jnp.tile(coarse_perm, 6) * 6 + faces
    their_id = ordered % count * 6 + faces + 1 - 2 * (faces % 2)
    key = jnp.where(me < target, own_id, their_id)
    which = jnp.sum(
        (target[:, None] == target[None, :]) & (key[None, :] < key[:, None]),
        axis=1,
        dtype=jnp.int32,
    )
    to = (target - me + devices - 1) % devices
    come = (me - target + devices - 1) % devices
    item_ids = jnp.arange(6 * count, dtype=jnp.int32)
    slot_ids = jnp.arange(2 * devices, dtype=jnp.int32)
    slots = jnp.sum(
        jnp.where((2 * to + which)[None, :] == slot_ids[:, None], item_ids[None, :], 0),
        axis=1,
        dtype=jnp.int32,
    )
    mask = jnp.broadcast_to(which.astype(F32).reshape(12, 8, 1), (12, 8, 128))
    return inverse(place), place, slots, come, which, mask


def local(fluid_state, neighbours, parents):
    level = lax.axis_index("level")
    me = lax.axis_index("blk")
    devices = lax.axis_size("blk")
    count = fluid_state.shape[1]
    perm, place, slots, where, which, mask = tables(
        neighbours, parents, level, me, count, devices
    )
    smem = pl.BlockSpec(memory_space=pltpu.SMEM)
    vmem = pl.BlockSpec(memory_space=pltpu.VMEM)
    peers = devices - 1

    def step(*refs):
        step_kernel(devices, *refs)

    result = pl.pallas_call(
        step,
        out_shape=jax.ShapeDtypeStruct(fluid_state.shape[1:], F32),
        in_specs=[smem] * 4 + [vmem] * 2,
        out_specs=vmem,
        scratch_shapes=[
            pltpu.VMEM((3, 5, 16, 4, 8, 128), F32),
            pltpu.VMEM((3, 5, 16, 4, 8, 128), F32),
            pltpu.VMEM((6, 5, 2, 4, 8, 128), F32),
            pltpu.VMEM((6, 5, 4, 8, 128), F32),
            pltpu.VMEM((96, 5, 8, 128), F32),
            pltpu.VMEM((96, 5, 4, 128), F32),
            pltpu.VMEM((96, 5, 4, 128), F32),
            pltpu.VMEM((peers, 5, 8, 128), F32),
            pltpu.VMEM((peers, 5, 8, 128), F32),
            pltpu.VMEM((peers, 5, 4, 128), F32),
            pltpu.VMEM((peers, 5, 4, 128), F32),
            pltpu.VMEM((peers, 5, 4, 128), F32),
            pltpu.VMEM((peers, 5, 4, 128), F32),
            pltpu.VMEM((6, 5, 4, 128), F32),
            pltpu.VMEM((6, 5, 4, 128), F32),
            pltpu.VMEM((6, 5, 4, 128), F32),
            pltpu.VMEM((6, 5, 4, 128), F32),
            pltpu.VMEM((2, 5, 2, 2, 8, 128), F32),
            pltpu.VMEM((2, 5, 2, 2, 8, 128), F32),
            pltpu.VMEM((6, 5, 4, 128), F32),
            pltpu.VMEM((6, 5, 4, 128), F32),
            pltpu.SemaphoreType.DMA((3,)),
            pltpu.SemaphoreType.DMA((3,)),
            pltpu.SemaphoreType.DMA((4,)),
            pltpu.SemaphoreType.DMA((4,)),
        ],
        compiler_params=pltpu.CompilerParams(
            collective_id=0, has_side_effects=True, vmem_limit_bytes=60 * 1024 * 1024
        ),
    )(perm, slots, where, which, fluid_state, mask)
    return pl.pallas_call(
        place_kernel,
        out_shape=jax.ShapeDtypeStruct(fluid_state.shape, F32),
        in_specs=[smem, vmem],
        out_specs=vmem,
    )(place, result)


def solution(mesh):
    return jax.shard_map(
        local,
        mesh=mesh,
        in_specs=(P("level", "blk", None, None, None), P(), P()),
        out_specs=P("level", "blk", None, None, None),
        check_vma=False,
    )
```

time: 932 us -> 189 us (0.20); the launches traced: 915 us -> 188 us
  local copies, waits for them, and re-layouts: 543 us -> 1.89 us
  waiting for transfers between devices: 239 us -> 0 us
  Pallas kernels: 0 us -> 183 us
  other arithmetic: 68.3 us -> 2.76 us
  starting transfers between devices: 51.8 us -> 0 us
  loops' own time: 10.3 us -> 0 us
    pallas_call x0 -> x2, Pallas kernels: none -> 183 us  [the longest x1 180 us: local(): pl.pallas_call(step, out_shape=jax.ShapeDtypeStruct(fluid_state.shape[1:]...]
    reshape x32 -> x2, local copies, waits for them, and re-layouts: 162 us -> 0.16 us  [the longest x1 0.08 us: tables(): faces = jnp.repeat(jnp.arange(6, dtype=jnp.int32), count)]
    ppermute x3 -> x0, waiting for transfers between devices: 140 us -> none  [shifted(): return lax.ppermute(array, axis, pairs)]
    gather x64 -> x0, local copies, waits for them, and re-layouts: 126 us -> none  [the longest x2 51.2 us: local(): neighbours.reshape(-1)]
    transpose x16 -> x0, local copies, waits for them, and re-layouts: 102 us -> none  [the longest x2 27.9 us: oriented(): cube_cells = cube_cells.transpose(0, 1, 3, 2, 4)]
    all_to_all x3 -> x0, waiting for transfers between devices: 99.4 us -> none  [route(): lax.all_to_all(buffer, 'blk', split_axis=0, concat_axis=0, tiled=True)]
    all_to_all x3 -> x0, starting transfers between devices: 47.1 us -> none  [route(): lax.all_to_all(buffer, 'blk', split_axis=0, concat_axis=0, tiled=True)]
    another operation x31 -> x1, local copies, waits for them, and re-layouts: 41.8 us -> 0.01 us  [tables(): own_id = jnp.tile(coarse_perm, 6) * 6 + faces]
  transfers between devices with their start and end apart: 6 -> 0, of which waited for: 4 -> 0; matrix products, arithmetic and copies ran while one was open for 8% -> 0% of each run, Pallas kernels for 0% -> 0%
where the time goes in v1:
time: 189 us; the launch traced here: 188 us
  Pallas kernels  183 us (97%)
  other arithmetic  2.76 us (1%)
    pallas_call x1, Pallas kernels, local(): pl.pallas_call(step, out_shape=jax.ShapeDtypeStruct(fluid_state.shape[1:]...  180 us

profile of v1, /device:TPU:2, one launch (start us, length us, event | category | flops | bytes accessed | tf_op | source)
XLA Modules:
  0.0 187.6 jit_solution(7881410525031586731)
XLA Ops:
  0.0 0.0 copy-start
  0.0 0.8 constant_dynamic-slice_fusion.1
  0.8 0.1 fusion
  0.9 0.1 convert_reduce_fusion.1
  1.0 0.2 select_reduce_fusion.4
  1.2 0.0 copy-start.2
  1.2 0.7 select_reduce_fusion.2
  1.9 0.1 iota_compare_fusion.1
  2.0 0.1 mul.71
  2.1 0.0 copy-done
  2.1 0.1 constant_dynamic-slice_fusion
  2.1 0.2 select_reduce_fusion.1
  2.3 0.1 reshape.293
  2.4 0.5 and_select_fusion
  3.0 0.1 reshape.294
  3.1 0.2 convert_reduce_fusion.refs_3_
  3.2 0.0 copy-start.1
  3.3 0.6 select_reduce_fusion.refs_1_
  3.9 0.1 convert_element_type.19
  4.0 0.7 broadcast_in_dim.95.refs_5_
  4.7 0.0 copy-done.1
  4.7 180.3 %shard_map.37.source = f32[16,5,16,256]{3,2,1,0:T(8,128)} custom-call(s32[16]{0:T(128)} %get-tuple-element.12.refs_0_, s32[256]{0:T(256)} %select_reduce_fusion.refs_1_, s32[96]{0:T(128)} %get-tuple-element.5.refs_2_, s32[96]{0:T(128)} %copy-done.1, f32[1,16,5,16,256]{4,3,2,1,0:T(8,128)} %refs_4_.1, f32[12,8,128]{2,1,0:T(8,128)} %broadcast_in_dim.95.refs_5_), custom_call_target="tpu_custom_call" | custom-call | tf_op jit(solution)/shard_map/pallas_call | solution.py:704
  185.0 0.0 copy-done.2
  185.0 2.6 %shard_map.38 = f32[1,16,5,16,256]{4,3,2,1,0:T(8,128)} custom-call(s32[16]{0:T(128)} %copy-done.2, f32[16,5,16,256]{3,2,1,0:T(8,128)} %shard_map.37.source), custom_call_target="tpu_custom_call" | custom-call | tf_op jit(solution)/shard_map/pallas_call | solution.py:740
  (7 shorter events, 0.1 us)
Async XLA Ops:
  0.0 2.1 %copy-start = (s32[2048,6]{0,1:T(8,128)S(1)}, s32[2048,6]{0,1:T(8,128)}, u32[]{:S(2)}) copy-start(s32[2048,6]{0,1:T(8,128)} %param.4) | copy-start | bytes 147460
  1.2 183.8 %copy-start.2 = (s32[16]{0:T(128)}, s32[16]{0:T(128)S(1)}, u32[]{:S(2)}) copy-start(s32[16]{0:T(128)S(1)} %get-tuple-element.7.back) | copy-start | bytes 196
  3.2 1.5 copy-start.1

commit v2 on v1

v2 whole, which is shorter than its diff:
```python
import jax
import jax.numpy as jnp
from jax import lax
from jax.experimental import pallas as pl
from jax.experimental.pallas import tpu as pltpu
from jax.sharding import PartitionSpec as P

GAMMA = 1.4
RATIO = 0.12
MESH = pl.DeviceIdType.MESH
ORDER = ((0, 1, 2, 3, 4), (0, 2, 1, 3, 4), (0, 3, 1, 2, 4))
BIT_OF = (4, 2, 1)
TANGENT = ((2, 1), (1, 4), (2, 4))
F32 = jnp.float32


def iota(axis):
    return lax.broadcasted_iota(jnp.int32, (8, 128), axis)


def take(tile, index):
    return jnp.take_along_axis(tile, index, axis=1, mode="promise_in_bounds")


def flip8(tiles):
    return jnp.swapaxes(jnp.stack(tiles), 0, 1)


def turn(tiles):
    whole = jnp.concatenate(tiles, axis=0).T
    return [whole[8 * i : 8 * i + 8] for i in range(16)]


def halves(tile):
    lane = iota(1)
    other = pltpu.roll(tile, 64, 1)
    return jnp.where(lane < 64, tile, other), jnp.where(lane < 64, other, tile)


def join(low, high, second):
    lane = iota(1)
    low = jnp.where(second, pltpu.roll(low, 64, 1), low)
    high = jnp.where(second, high, pltpu.roll(high, 64, 1))
    return jnp.where(lane < 64, low, high)


def prim(q):
    inverse = 1.0 / q[0]
    speed = q[1] * inverse
    kinetic = (q[1] * q[1] + q[2] * q[2] + q[3] * q[3]) * inverse
    return inverse, speed, (GAMMA - 1.0) * (q[4] - 0.5 * kinetic)


def flux_of(q, speed, pressure):
    return [q[1], q[1] * speed + pressure, q[2] * speed, q[3] * speed, (q[4] + pressure) * speed]


def half_step(below, here, above, low_wanted=True, high_wanted=True):
    low, high = [], []
    for u0, u1, u2 in zip(below, here, above):
        a = u1 - u0
        b = u2 - u1
        slope = jnp.maximum(jnp.minimum(a, b), 0.0) + jnp.minimum(jnp.maximum(a, b), 0.0)
        low.append(u1 - 0.5 * slope)
        high.append(u1 + 0.5 * slope)
    _, speed, pressure = prim(low)
    flux_low = flux_of(low, speed, pressure)
    _, speed, pressure = prim(high)
    flux_high = flux_of(high, speed, pressure)
    change = [0.5 * RATIO * (a - b) for a, b in zip(flux_low, flux_high)]
    low = [a + b for a, b in zip(low, change)] if low_wanted else None
    high = [a + b for a, b in zip(high, change)] if high_wanted else None
    return low, high


def with_sound(q):
    inverse, speed, pressure = prim(q)
    return q, inverse, speed, pressure, jnp.sqrt(GAMMA * pressure * inverse)


def contact_flux(low, high):
    ql, il, ul, pl_, cl = with_sound(low)
    qh, ih, uh, ph, ch = with_sound(high)
    slowest = jnp.minimum(ul - cl, uh - ch)
    fastest = jnp.maximum(ul + cl, uh + ch)
    mass_l = ql[0] * (slowest - ul)
    mass_h = qh[0] * (fastest - uh)
    contact = (ph - pl_ + ul * mass_l - uh * mass_h) / (mass_l - mass_h)
    lower = jnp.logical_or(slowest >= 0.0, contact >= 0.0)
    q = [jnp.where(lower, a, b) for a, b in zip(ql, qh)]
    inverse = jnp.where(lower, il, ih)
    speed = jnp.where(lower, ul, uh)
    pressure = jnp.where(lower, pl_, ph)
    mass = jnp.where(lower, mass_l, mass_h)
    wave = jnp.where(lower, slowest, fastest)
    outside = jnp.logical_or(slowest >= 0.0, jnp.logical_and(contact < 0.0, fastest <= 0.0))
    flux = flux_of(q, speed, pressure)
    over = 1.0 / (wave - contact)
    factor = mass * over
    scaled = factor * inverse
    gap = contact - speed
    star = [
        factor,
        factor * contact,
        scaled * q[2],
        scaled * q[3],
        scaled * q[4] + gap * (factor * contact + pressure * over),
    ]
    return [jnp.where(outside, f, f + wave * (s - u)) for f, s, u in zip(flux, star, q)]


def cells(V, a, i, ch):
    return [V[a, c, i, ch] for c in range(5)]


def ghost(G, a, s, layer, ch):
    return [G[2 * a + s, c, layer, ch] for c in range(5)]


def inner_sweep(V, D):
    def body(n, carry):
        a = n // 4
        ch = n % 4
        states = [cells(V, a, i, ch) for i in range(3)]
        _, high = half_step(*states)
        previous = None
        for i in range(2, 15):
            states = [states[1], states[2], cells(V, a, i + 1, ch)]
            low, next_high = half_step(*states)
            flux = contact_flux(high, low)
            for c in range(5):
                D[a, c, i - 1, ch] = flux[c] if previous is None else flux[c] - previous[c]
            high, previous = next_high, flux
        for c in range(5):
            D[a, c, 14, ch] = -previous[c]
        return carry

    lax.fori_loop(0, 12, body, 0)


def outer_sweep(V, G, D, FC, first):
    def body(n, carry):
        a = n // 4
        ch = n % 4
        u = [cells(V, a, i, ch) for i in range(3)]
        g = [ghost(G, a, 0, layer, ch) for layer in range(2)]
        _, r_ghost = half_step(g[0], g[1], u[0], low_wanted=False)
        l0, r0 = half_step(g[1], u[0], u[1])
        l1, _ = half_step(u[0], u[1], u[2], high_wanted=False)
        f0 = contact_flux(r_ghost, l0)
        f1 = contact_flux(r0, l1)
        for c in range(5):
            D[a, c, 0, ch] = f1[c] - f0[c]
            D[a, c, 1, ch] = D[a, c, 1, ch] - f1[c]
            FC[2 * a, c, ch] = f0[c] if first else FC[2 * a, c, ch] + f0[c]
        u = [cells(V, a, i, ch) for i in (13, 14, 15)]
        g = [ghost(G, a, 1, layer, ch) for layer in range(2)]
        _, r0 = half_step(u[0], u[1], u[2], low_wanted=False)
        l1, r1 = half_step(u[1], u[2], g[0])
        l2, _ = half_step(u[2], g[0], g[1], high_wanted=False)
        f0 = contact_flux(r0, l1)
        f1 = contact_flux(r1, l2)
        for c in range(5):
            D[a, c, 14, ch] = D[a, c, 14, ch] + f0[c]
            D[a, c, 15, ch] = f1[c] - f0[c]
            FC[2 * a + 1, c, ch] = f1[c] if first else FC[2 * a + 1, c, ch] + f1[c]
        return carry

    lax.fori_loop(0, 12, body, 0)


def update(N, D):
    def body(n, carry):
        X = n // 2
        h = n % 2
        for c in range(5):
            c1, c2 = ORDER[1].index(c), ORDER[2].index(c)
            tiles = [None] * 16
            for z in range(2):
                rows = flip8([D[2, c2, 8 * z + i, 2 * h + X] for i in range(8)])
                for y in range(8):
                    tiles[2 * y + z] = D[1, c1, 8 * h + y, 2 * z + X] + rows[y]
            tiles = turn(tiles)
            for t in range(2):
                rows = flip8([D[0, c, 8 * X + i, 2 * h + t] for i in range(8)])
                for j in range(8):
                    q = 8 * t + j
                    N[q, c, X, h] = N[q, c, X, h] - RATIO * (tiles[q] + rows[j])
        return carry

    lax.fori_loop(0, 4, body, 0)


def make_views(N, V, fluid=None, perm=None):
    def body(n, carry):
        X = n // 2
        h = n % 2
        for c in range(5):
            c1, c2 = ORDER[1].index(c), ORDER[2].index(c)
            tiles = []
            for q in range(16):
                if fluid is None:
                    tiles.append(N[q, c, X, h])
                else:
                    rows = pl.ds(pl.multiple_of(8 * X, 8), 8)
                    lanes = pl.ds(pl.multiple_of(128 * h, 128), 128)
                    tiles.append(fluid[0, perm[q], c, rows, lanes])
                    N[q, c, X, h] = tiles[q]
            for t in range(2):
                rows = flip8(tiles[8 * t : 8 * t + 8])
                for i in range(8):
                    V[0, c, 8 * X + i, 2 * h + t] = rows[i]
            tiles = turn(tiles)
            for z in range(2):
                for y in range(8):
                    V[1, c1, 8 * h + y, 2 * z + X] = tiles[2 * y + z]
                rows = flip8([tiles[2 * y + z] for y in range(8)])
                for i in range(8):
                    V[2, c2, 8 * z + i, 2 * h + X] = rows[i]
        return carry

    lax.fori_loop(0, 4, body, 0)


def store_state(N, out):
    def body(q, carry):
        for c in range(5):
            for X in range(2):
                for h in range(2):
                    out[q, c, 8 * X : 8 * X + 8, 128 * h : 128 * h + 128] = N[q, c, X, h]
        return carry

    lax.fori_loop(0, 16, body, 0)


def make_slabs(V, items):
    def x_body(n, carry):
        s = n // 2
        t = n % 2
        codes = [
            [V[0, c, 14 * s + layer, 2 * h + t] for layer in range(2) for h in range(2)]
            for c in range(5)
        ]
        last = [half for tile in codes[4] for half in halves(tile)]
        for g, tiles in enumerate((codes[0] + codes[1], codes[2] + codes[3], last)):
            rows = flip8(tiles)
            for j in range(8):
                items[s * 16 + 8 * t + j, g] = rows[j]
        return carry

    def body(n, carry):
        a = 1 + n // 2
        s = n % 2
        codes = [
            [V[a, c, 14 * s + layer, k] for layer in range(2) for k in range(4)] for c in range(5)
        ]
        for g, tiles in enumerate((codes[0] + codes[1], codes[2] + codes[3], codes[4] * 2)):
            tiles = turn(tiles)
            for q in range(16):
                items[(2 + n) * 16 + q, g] = tiles[q]
        return carry

    lax.fori_loop(0, 4, x_body, 0)
    lax.fori_loop(0, 4, body, 0)


def make_rims(V, items):
    def x_body(n, carry):
        s = n // 2
        t = n % 2
        codes = [[V[0, c, 15 * s, 2 * h + t] for h in range(2)] for c in range(5)]
        last = [half for tile in codes[4] for half in halves(tile)]
        for g, tiles in enumerate((codes[0] + codes[1] + codes[2] + codes[3], last * 2)):
            rows = flip8(tiles)
            for j in range(8):
                items[s * 16 + 8 * t + j, g] = rows[j]
        return carry

    def body(n, carry):
        a = 1 + n // 2
        s = n % 2
        codes = [[V[a, c, 15 * s, k] for k in range(4)] for c in range(5)]
        for g, tiles in enumerate((codes[0] + codes[1] + codes[2] + codes[3], codes[4] * 4)):
            tiles = turn(tiles)
            for q in range(16):
                items[(2 + n) * 16 + q, g] = tiles[q]
        return carry

    lax.fori_loop(0, 4, x_body, 0)
    lax.fori_loop(0, 4, body, 0)


def pack(items, slots, send):
    whole = items.shape[1] - 1

    def body(d, carry):
        lane = iota(1)
        i0 = slots[2 * d]
        i1 = slots[2 * d + 1]
        for g in range(whole):
            send[d, g] = items[i0, g]
            send[d, whole + g] = items[i1, g]
        send[d, 2 * whole] = jnp.where(lane < 64, items[i0, whole], items[i1, whole])
        return carry

    lax.fori_loop(0, send.shape[0], body, 0)


def collect_slabs(recv, where, which, row_mask, lane_mask, G):
    def x_body(n, carry):
        s = n // 2
        t = n % 2
        second = row_mask[n] > 0.5
        first = s * 16 + 8 * t
        for g in range(2):
            rows = flip8([recv[where[first + j], 2 * which[first + j] + g] for j in range(8)])
            for m in range(8):
                c, layer, h = 2 * g + m // 4, m // 2 % 2, m % 2
                G[s, c, layer, 2 * h + t] = rows[m]
        rows = flip8([recv[where[first + j], 4] for j in range(8)])
        for layer in range(2):
            for h in range(2):
                m = 2 * layer + h
                G[s, 4, layer, 2 * h + t] = join(rows[2 * m], rows[2 * m + 1], second)
        return carry

    def body(n, carry):
        second = lane_mask[n] > 0.5
        first = (2 + n) * 16
        for g in range(2):
            tiles = turn([recv[where[first + q], 2 * which[first + q] + g] for q in range(16)])
            for m in range(16):
                G[2 + n, 2 * g + m // 8, m // 4 % 2, m % 4] = tiles[m]
        tiles = turn([recv[where[first + q], 4] for q in range(16)])
        for m in range(8):
            G[2 + n, 4, m // 4, m % 4] = jnp.where(second, tiles[8 + m], tiles[m])
        return carry

    lax.fori_loop(0, 4, x_body, 0)
    lax.fori_loop(0, 4, body, 0)


def early_rims(G, rims):
    face = iota(1) // 8 % 8

    def body(c, carry):
        for k in range(4):
            tile = G[2, c, 1, k]
            for n in range(1, 4):
                tile = jnp.where(face == n, pltpu.roll(G[2 + n, c, 1 - n % 2, k], 8 * n, 1), tile)
            rims[4 * c + k] = tile
        for f in range(2):
            for t in range(2):
                for h in range(2):
                    r = 4 * f + 2 * t + h
                    rims[20 + c, r : r + 1, :] = G[f, c, 1 - f, 2 * h + t, 0:1, :]
        return carry

    lax.fori_loop(0, 5, body, 0)


def late_rims(recv, where, which, lane_mask, rims):
    for f in range(2):
        for t in range(2):
            item = f * 16 + 8 * t
            r = 4 * f + 2 * t
            tile = recv[where[item], which[item]]
            for c in range(4):
                rims[20 + c, r : r + 2, :] = tile[2 * c : 2 * c + 2]
            tile = recv[where[item], 2]
            joined = join(tile, pltpu.roll(tile, 7, 0), which[item] == 1)
            for h in range(2):
                rims[24, r + h : r + h + 1, :] = joined[2 * h : 2 * h + 1]
    items = [f * 16 + 8 * t for t in range(2) for _ in range(2) for f in range(2, 6)]
    tiles = turn([recv[where[i], which[i]] for i in items])
    for m in range(16):
        rims[m] = tiles[m]
    tiles = turn([recv[where[i], 2] for i in items])
    for m in range(4):
        rims[16 + m] = jnp.where(lane_mask[4] > 0.5, tiles[8 + m], tiles[m])


def spread_rows(tile, u):
    sub = iota(0)
    result = pltpu.roll(tile, 4, 0) if u else tile
    base = result
    for r in range(1, 5):
        result = jnp.where((sub + 1) // 2 == r, pltpu.roll(base, r, 0), result)
    return result


def fine_ghosts(V, rims, G, late=None):
    lane = iota(1)
    sub = iota(0)

    def rim(*index):
        value = rims[index]
        return value if late is None else 0.5 * (value + late[index])

    for f in range(2):
        outer = (sub // 4) % 2 == f
        first = (sub // 2) % 2 == 1
        second = sub % 2

        def x_body(c, carry):
            for t in range(2):
                r = 4 * f + 2 * t
                row = [
                    jnp.broadcast_to(rim(20 + c, pl.ds(r + h, 1), slice(None)), (8, 128))
                    for h in range(2)
                ]
                source = jnp.where(first, row[1], row[0])
                for h in range(2):
                    index = (4 * h + lane // 32) * 16 + 8 * second + (lane % 16) // 2
                    coarse = take(source, index)
                    for layer in range(2):
                        near = V[0, c, (layer if f else 14 + layer), 2 * h + t]
                        near = pltpu.roll(near, 4, 0)
                        G[f, c, layer, 2 * h + t] = jnp.where(outer, coarse, near)
            return carry

        lax.fori_loop(0, 5, x_body, 0)

    octant = lane // 8 % 8
    for f in range(2, 6):
        a, s = f // 2, f % 2
        bit = BIT_OF[a]
        outer = octant // bit % 2 == s
        first = octant // TANGENT[a][0] % 2 == 1
        second = octant // 4 == 1

        def body(c, carry):
            source = [rim(4 * c + k) for k in range(4)]
            for X in range(2):
                index = (lane // 64 * 8 + f - 2) * 8 + 4 * X + lane % 8 // 2
                four = [take(tile, index) for tile in source]
                low = jnp.where(second, four[1], four[0])
                high = jnp.where(second, four[3], four[2])
                chosen = jnp.where(first, high, low)
                for u in range(2):
                    coarse = spread_rows(chosen, u)
                    for layer in range(2):
                        near = V[a, c, (layer if s else 14 + layer), 2 * u + X]
                        near = pltpu.roll(near, (128 - 8 * bit) if s else 8 * bit, 1)
                        G[f, c, layer, 2 * u + X] = jnp.where(outer, coarse, near)
            return carry

        lax.fori_loop(0, 5, body, 0)


def pair_sums(low, high):
    lane = iota(1)
    index = (lane // 16 % 4) * 32 + 2 * (lane % 8)
    sums = []
    for tile in (low, high):
        tile = tile + pltpu.roll(tile, 127, 1)
        sums.append(take(tile + pltpu.roll(tile, 112, 1), index))
    merged = jnp.where(lane < 64, sums[0], sums[1])
    return jnp.where(lane % 16 < 8, merged, pltpu.roll(merged, 7, 0))


def restrict_cells(N, mixed):
    def body(n, carry):
        t = n % 2
        c = n // 2
        merged = []
        for X in range(2):
            rows = [flip8([N[8 * t + j, c, X, h] for j in range(8)]) for h in range(2)]
            for x in range(4):
                low, high = [rows[h][2 * x] + rows[h][2 * x + 1] for h in range(2)]
                merged.append(pair_sums(low, high) * 0.125)
        rows = flip8(merged)
        for X in range(2):
            for h in range(2):
                mixed[t, c, X, h] = rows[4 * X + 2 * h]
        return carry

    lax.fori_loop(0, 10, body, 0)


def restrict_faces(FC, means):
    lane = iota(1)
    sub = iota(0)

    def x_body(c, carry):
        for f in range(2):
            for t in range(2):
                merged = pair_sums(FC[f, c, t], FC[f, c, 2 + t]) * 0.125
                for h in range(2):
                    o = 4 * f + 2 * h
                    r = 4 * f + 2 * t + h
                    means[20 + c, r : r + 1, :] = merged[o : o + 1]
        return carry

    def body(c, carry):
        index = lane // 8 * 8 + 2 * (lane % 4)
        for n in range(4):
            result = None
            for u in range(2):
                sums = []
                for X in range(2):
                    tile = FC[2 + n, c, 2 * u + X]
                    tile = tile + pltpu.roll(tile, 127, 1)
                    sums.append(take(tile + pltpu.roll(tile, 7, 0), index))
                merged = jnp.where(lane % 8 < 4, sums[0], sums[1])
                for i in range(4):
                    moved = pltpu.roll(merged, (8 - i) % 8, 0) if u == 0 else pltpu.roll(merged, 4 - i, 0)
                    if result is None:
                        result = moved
                    else:
                        result = jnp.where(sub == 4 * u + i, moved, result)
            means[5 * n + c] = result * 0.125
        return carry

    lax.fori_loop(0, 5, x_body, 0)
    lax.fori_loop(0, 5, body, 0)


def make_deltas(FC, means, items):
    lane = lax.broadcasted_iota(jnp.int32, (1, 128), 1)
    for f in range(2):
        for t in range(2):
            item = f * 16 + 8 * t
            for c in range(5):
                for h in range(2):
                    r = 4 * f + 2 * t + h
                    delta = FC[f, c, 2 * h + t, 0:1, :] - means[20 + c, r : r + 1, :]
                    if c < 4:
                        items[item, 0, 2 * c + h : 2 * c + h + 1, :] = delta
                    else:
                        other = pltpu.roll(delta, 64, 1)
                        items[item, 1, 2 * h : 2 * h + 1, :] = jnp.where(lane < 64, delta, other)
                        items[item, 1, 2 * h + 1 : 2 * h + 2, :] = jnp.where(
                            lane < 64, other, delta
                        )
    for n in range(4):
        a, s = 1 + n // 2, n % 2
        codes = []
        for c in range(5):
            fine = means[5 * n + c]
            for k in range(4):
                o = s * BIT_OF[a] + (k // 2) * TANGENT[a][0] + (k % 2) * 4
                codes.append(FC[2 + n, c, k] - pltpu.roll(fine, (128 - 8 * o) % 128, 1))
        for g, tiles in enumerate((codes[:16], codes[16:] * 4)):
            tiles = turn(tiles)
            for t in range(2):
                items[(2 + n) * 16 + 8 * t, g] = tiles[8 * t]


def take_mixed(N, mixed):
    def body(c, carry):
        for t in range(2):
            for X in range(2):
                for h in range(2):
                    N[8 * t, c, X, h] = mixed[t, c, X, h]
        return carry

    lax.fori_loop(0, 5, body, 0)


def apply_corrections(recv, where, which, lane_mask, change, N):
    sub = iota(0)

    def x_body(q, carry):
        for s in range(2):
            scale = RATIO if s else -RATIO
            item = s * 16 + q
            e = where[item]
            k = which[item]
            tile = recv[e, 2]
            joined = join(tile, pltpu.roll(tile, 7, 0), k == 1)
            tile = recv[e, k]
            for c in range(5):
                for h in range(2):
                    row = tile[2 * c + h : 2 * c + h + 1] if c < 4 else joined[2 * h : 2 * h + 1]
                    row = jnp.broadcast_to(scale * row, (8, 128))
                    N[q, c, s, h] = N[q, c, s, h] + jnp.where(sub == 7 * s, row, 0.0)
        return carry

    lax.fori_loop(0, 16, x_body, 0)

    for n in range(4):
        scale = RATIO if n % 2 else -RATIO
        first = (2 + n) * 16
        tiles = turn([recv[where[first + q], which[first + q]] for q in range(16)])
        for m in range(16):
            change[n, m // 4, m % 4] = scale * tiles[m]
        tiles = turn([recv[where[first + q], 2] for q in range(16)])
        for m in range(4):
            change[n, 4, m] = scale * jnp.where(lane_mask[n] > 0.5, tiles[8 + m], tiles[m])

    def body(X, carry):
        for c in range(5):
            c1, c2 = ORDER[1].index(c), ORDER[2].index(c)
            for h in range(2):
                tiles = []
                for y in range(8):
                    for z in range(2):
                        row = jnp.broadcast_to(
                            change[2 + z, c2, 2 * h + X, y : y + 1, :], (8, 128)
                        )
                        tile = jnp.where(sub == 7 * z, row, 0.0)
                        if y == 7 * h:
                            tile = tile + change[h, c1, 2 * z + X]
                        tiles.append(tile)
                tiles = turn(tiles)
                for q in range(16):
                    N[q, c, X, h] = N[q, c, X, h] + tiles[q]
        return carry

    lax.fori_loop(0, 2, body, 0)


def step_kernel(
    devices,
    perm,
    slots,
    where,
    which,
    fluid,
    row_mask,
    lane_mask,
    out,
    N,
    V,
    D,
    G,
    FC,
    change,
    items1,
    items2,
    items3,
    send1,
    recv1,
    send2,
    recv2,
    send3,
    recv3,
    early_out,
    early_in,
    late_out,
    late_in,
    mixed_out,
    mixed_in,
    means_out,
    means_in,
    send_sems,
    recv_sems,
    pair_send,
    pair_recv,
    ready,
):
    level = lax.axis_index("level")
    me = lax.axis_index("blk")
    other = 1 - level
    barrier = pltpu.get_barrier_semaphore()

    def start_all(send, recv, n):
        def body(k, carry):
            d = lax.rem(k * 53 + 26, devices - 1)
            pltpu.make_async_remote_copy(
                src_ref=send.at[d],
                dst_ref=recv.at[d],
                send_sem=send_sems.at[n],
                recv_sem=recv_sems.at[n],
                device_id=(level, lax.rem(me + d + 1, devices)),
                device_id_type=MESH,
            ).start()
            return carry

        lax.fori_loop(0, devices - 1, body, 0)

    def whole(send, recv, n):
        return pltpu.make_async_remote_copy(
            src_ref=send,
            dst_ref=recv,
            send_sem=send_sems.at[n],
            recv_sem=recv_sems.at[n],
            device_id=(level, lax.rem(me + 1, devices)),
            device_id_type=MESH,
        )

    def to_pair(source, target, n):
        return pltpu.make_async_remote_copy(
            src_ref=source,
            dst_ref=target,
            send_sem=pair_send.at[n],
            recv_sem=pair_recv.at[n],
            device_id=(other, me),
            device_id_type=MESH,
        )

    def greet(semaphore, peers):
        for peer in peers:
            pl.semaphore_signal(
                semaphore, inc=1, device_id=(level, peer), device_id_type=MESH
            )

    plane = devices // 8
    far, mid, near = me // plane, me // 4 % 4, me % 4
    line_far = [lax.rem(far + i, 8) * plane + me % plane for i in range(1, 8)]
    line_mid = [far * plane + lax.rem(mid + i, 4) * 4 + near for i in range(1, 4)]
    line_near = [far * plane + mid * 4 + lax.rem(near + i, 4) for i in range(1, 4)]

    pl.semaphore_signal(barrier, inc=1, device_id=(other, me), device_id_type=MESH)

    @pl.when(level == 0)
    def _():
        greet(barrier, line_far + line_mid + line_near)

    make_views(N, V, fluid, perm)

    @pl.when(level == 0)
    def _():
        pl.semaphore_wait(barrier, 14)
        greet(ready.at[0], line_far)
        make_slabs(V, items1)
        pl.semaphore_wait(ready.at[0], 7)
        greet(ready.at[1], line_mid)
        pack(items1, slots, send1)
        pl.semaphore_wait(ready.at[1], 3)
        start_all(send1, recv1, 0)

        def clear(n, carry):
            for g in range(2):
                items3[n, g] = jnp.zeros((8, 128), F32)
            return carry

        lax.fori_loop(0, 96, clear, 0)

    @pl.when(level == 1)
    def _():
        pl.semaphore_wait(barrier, 1)

    inner_sweep(V, D)

    @pl.when(level == 0)
    def _():
        whole(send1, recv1, 0).wait_recv()
        collect_slabs(recv1, where, which, row_mask, lane_mask, G)
        early_rims(G, early_out)
        to_pair(early_out, early_in, 0).start()

    @pl.when(level == 1)
    def _():
        to_pair(early_out, early_in, 0).wait_recv()
        fine_ghosts(V, early_in, G)

    outer_sweep(V, G, D, FC, True)
    update(N, D)
    make_views(N, V)

    @pl.when(level == 0)
    def _():
        make_rims(V, items2)
        pack(items2, slots, send2)
        start_all(send2, recv2, 1)
        whole(send2, recv2, 1).wait_recv()
        late_rims(recv2, where, which, lane_mask, late_out)
        to_pair(late_out, late_in, 1).start()

        to_pair(means_out, means_in, 3).wait_recv()
        make_deltas(FC, means_in, items3)
        pack(items3, slots, send3)
        start_all(send3, recv3, 2)
        to_pair(mixed_out, mixed_in, 2).wait_recv()
        take_mixed(N, mixed_in)
        whole(send3, recv3, 2).wait_recv()
        apply_corrections(recv3, where, which, lane_mask, change, N)

    @pl.when(level == 1)
    def _():
        inner_sweep(V, D)
        to_pair(late_out, late_in, 1).wait_recv()
        fine_ghosts(V, early_in, G, late_in)
        outer_sweep(V, G, D, FC, False)
        restrict_faces(FC, means_out)
        to_pair(means_out, means_in, 3).start()
        update(N, D)
        restrict_cells(N, mixed_out)
        to_pair(mixed_out, mixed_in, 2).start()

    store_state(N, out)

    @pl.when(level == 0)
    def _():
        whole(send1, recv1, 0).wait_send()
        whole(send2, recv2, 1).wait_send()
        whole(send3, recv3, 2).wait_send()
        to_pair(early_out, early_in, 0).wait_send()
        to_pair(late_out, late_in, 1).wait_send()

    @pl.when(level == 1)
    def _():
        to_pair(mixed_out, mixed_in, 2).wait_send()
        to_pair(means_out, means_in, 3).wait_send()


def place_kernel(back, source, out):
    def body(b, carry):
        out[0, b] = source[back[b]]
        return carry

    lax.fori_loop(0, out.shape[1], body, 0)


def tables(neighbours, parents, level, me, count, devices):
    rows = lax.dynamic_slice_in_dim(neighbours, me * count, count, 0)
    family = lax.dynamic_slice_in_dim(parents, me * count, count, 0)
    ids = jnp.arange(count, dtype=jnp.int32)
    owner = family[:, 0] - me * count
    owns = owner[:, None] == ids[None, :]
    is_parent = jnp.any(owns, axis=0)
    earlier = ids[None, :] < ids[:, None]
    parent_rank = jnp.sum(is_parent[None, :] & earlier, axis=1, dtype=jnp.int32)
    rest_rank = ids - parent_rank
    coarse_place = jnp.where(
        is_parent, 8 * parent_rank, jnp.where(rest_rank < 7, 1 + rest_rank, 2 + rest_rank)
    )
    fine_place = 8 * jnp.sum(jnp.where(owns, parent_rank[None, :], 0), axis=1) + family[:, 1]
    place = jnp.where(level == 0, coarse_place, fine_place).astype(jnp.int32)

    def inverse(position):
        return jnp.sum(
            jnp.where(position[None, :] == ids[:, None], ids[None, :], 0), axis=1, dtype=jnp.int32
        )

    coarse_perm = inverse(coarse_place)
    chosen = coarse_perm[:, None] == ids[None, :]
    ordered = jnp.sum(jnp.where(chosen[:, :, None], rows[None], 0), axis=1, dtype=jnp.int32)
    ordered = ordered.T.reshape(-1)
    faces = jnp.repeat(jnp.arange(6, dtype=jnp.int32), count)
    target = ordered // count
    own_id = jnp.tile(coarse_perm, 6) * 6 + faces
    their_id = ordered % count * 6 + faces + 1 - 2 * (faces % 2)
    key = jnp.where(me < target, own_id, their_id)
    which = jnp.sum(
        (target[:, None] == target[None, :]) & (key[None, :] < key[:, None]),
        axis=1,
        dtype=jnp.int32,
    )
    to = (target - me + devices - 1) % devices
    come = (me - target + devices - 1) % devices
    item_ids = jnp.arange(6 * count, dtype=jnp.int32)
    slot_ids = jnp.arange(2 * devices, dtype=jnp.int32)
    slots = jnp.sum(
        jnp.where((2 * to + which)[None, :] == slot_ids[:, None], item_ids[None, :], 0),
        axis=1,
        dtype=jnp.int32,
    )
    second = which.astype(F32).reshape(6, count)
    row_mask = jnp.broadcast_to(second[:2].reshape(4, 8, 1), (4, 8, 128))
    late = jnp.concatenate([second[2:, 0], second[2:, 0], second[2:, 8], second[2:, 8]])
    lanes = jnp.concatenate([second[2:], late[None]])
    lane_mask = jnp.broadcast_to(jnp.repeat(lanes, 8, axis=1)[:, None, :], (5, 8, 128))
    return inverse(place), place, slots, come, which, row_mask, lane_mask


def local(fluid_state, neighbours, parents):
    level = lax.axis_index("level")
    me = lax.axis_index("blk")
    devices = lax.axis_size("blk")
    count = fluid_state.shape[1]
    perm, place, slots, where, which, row_mask, lane_mask = tables(
        neighbours, parents, level, me, count, devices
    )
    smem = pl.BlockSpec(memory_space=pltpu.SMEM)
    vmem = pl.BlockSpec(memory_space=pltpu.VMEM)
    peers = devices - 1

    def step(*refs):
        step_kernel(devices, *refs)

    result = pl.pallas_call(
        step,
        out_shape=jax.ShapeDtypeStruct(fluid_state.shape[1:], F32),
        in_specs=[smem] * 4 + [vmem] * 3,
        out_specs=vmem,
        scratch_shapes=[
            pltpu.VMEM((16, 5, 2, 2, 8, 128), F32),
            pltpu.VMEM((3, 5, 16, 4, 8, 128), F32),
            pltpu.VMEM((3, 5, 16, 4, 8, 128), F32),
            pltpu.VMEM((6, 5, 2, 4, 8, 128), F32),
            pltpu.VMEM((6, 5, 4, 8, 128), F32),
            pltpu.VMEM((4, 5, 4, 8, 128), F32),
            pltpu.VMEM((96, 3, 8, 128), F32),
            pltpu.VMEM((96, 2, 8, 128), F32),
            pltpu.VMEM((96, 2, 8, 128), F32),
            pltpu.VMEM((peers, 5, 8, 128), F32),
            pltpu.VMEM((peers, 5, 8, 128), F32),
            pltpu.VMEM((peers, 3, 8, 128), F32),
            pltpu.VMEM((peers, 3, 8, 128), F32),
            pltpu.VMEM((peers, 3, 8, 128), F32),
            pltpu.VMEM((peers, 3, 8, 128), F32),
            pltpu.VMEM((25, 8, 128), F32),
            pltpu.VMEM((25, 8, 128), F32),
            pltpu.VMEM((25, 8, 128), F32),
            pltpu.VMEM((25, 8, 128), F32),
            pltpu.VMEM((2, 5, 2, 2, 8, 128), F32),
            pltpu.VMEM((2, 5, 2, 2, 8, 128), F32),
            pltpu.VMEM((25, 8, 128), F32),
            pltpu.VMEM((25, 8, 128), F32),
            pltpu.SemaphoreType.DMA((3,)),
            pltpu.SemaphoreType.DMA((3,)),
            pltpu.SemaphoreType.DMA((4,)),
            pltpu.SemaphoreType.DMA((4,)),
            pltpu.SemaphoreType.REGULAR((2,)),
        ],
        compiler_params=pltpu.CompilerParams(
            collective_id=0, has_side_effects=True, vmem_limit_bytes=60 * 1024 * 1024
        ),
    )(perm, slots, where, which, fluid_state, row_mask, lane_mask)
    return pl.pallas_call(
        place_kernel,
        out_shape=jax.ShapeDtypeStruct(fluid_state.shape, F32),
        in_specs=[smem, vmem],
        out_specs=vmem,
    )(place, result)


def solution(mesh):
    return jax.shard_map(
        local,
        mesh=mesh,
        in_specs=(P("level", "blk", None, None, None), P(), P()),
        out_specs=P("level", "blk", None, None, None),
        check_vma=False,
    )
```

time: 189 us -> 123 us (0.65)
  Pallas kernels: 183 us -> 116 us
    pallas_call x1, Pallas kernels: 180 us -> 113 us  [local(): pl.pallas_call(step, out_shape=jax.ShapeDtypeStruct(fluid_state.shape[1:]...]
where the time goes in v2:
time: 123 us; the launch traced here: 122 us
  Pallas kernels  116 us (94%)
  local copies, waits for them, and re-layouts  3.05 us (2%)
  other arithmetic  2.8 us (2%)
    pallas_call x1, Pallas kernels, local(): pl.pallas_call(step, out_shape=jax.ShapeDtypeStruct(fluid_state.shape[1:]...  113 us
    pallas_call x1, Pallas kernels, local(): pl.pallas_call(place_kernel, out_shape=jax.ShapeDtypeStruct(fluid_state.s...  2.55 us

profile of v2, /device:TPU:2, one launch (start us, length us, event | category | flops | bytes accessed | tf_op | source)
XLA Modules:
  0.0 121.5 jit_solution(14554248365245733018)
XLA Ops:
  0.0 0.0 copy-start
  0.0 0.8 constant_dynamic-slice_fusion.1
  0.8 0.1 fusion
  0.9 0.1 convert_reduce_fusion.1
  1.0 0.2 select_reduce_fusion.4
  1.2 0.0 copy-start.2
  1.2 0.6 select_reduce_fusion.2
  1.8 0.1 iota_compare_fusion.1
  1.9 0.1 mul.71
  2.0 0.0 copy-done
  2.0 0.1 constant_dynamic-slice_fusion
  2.1 0.2 select_reduce_fusion.1
  2.3 0.1 reshape.311
  2.3 0.6 and_select_fusion
  2.9 0.1 reshape.312
  3.0 0.2 convert_reduce_fusion.refs_3_
  3.2 0.0 copy-start.1
  3.2 0.6 select_reduce_fusion.refs_1_
  3.9 0.1 slice.31
  3.9 0.1 slice.32
  4.0 0.1 broadcast_in_dim.110
  4.1 0.1 convert_element_type.25
  4.2 0.2 slice_reduce_fusion.1
  4.4 0.1 maximum_bitcast_fusion
  4.5 0.7 broadcast_in_dim.111.refs_5_
  5.1 0.1 broadcast_in_dim.113
  5.2 0.1 broadcast_in_dim.114
  5.3 0.6 broadcast_in_dim.115.refs_6_
  5.9 0.0 copy-done.1
  5.9 113.0 %shard_map.37.source = f32[16,5,16,256]{3,2,1,0:T(8,128)} custom-call(s32[16]{0:T(128)} %get-tuple-element.14.refs_0_, s32[256]{0:T(256)} %select_reduce_fusion.refs_1_, s32[96]{0:T(128)} %get-tuple-element.7.refs_2_, s32[96]{0:T(128)} %copy-done.1, f32[1,16,5,16,256]{4,3,2,1,0:T(8,128)} %refs_4_.1, f32[4,8,128]{2,1,0:T(8,128)} %broadcast_in_dim.111.refs_5_, ...), custom_call_target="tpu_custom_call" | custom-call | tf_op jit(solution)/shard_map/pallas_call | solution.py:874
  119.0 0.0 copy-done.2
  119.0 2.6 %shard_map.38 = f32[1,16,5,16,256]{4,3,2,1,0:T(8,128)} custom-call(s32[16]{0:T(128)} %copy-done.2, f32[16,5,16,256]{3,2,1,0:T(8,128)} %shard_map.37.source), custom_call_target="tpu_custom_call" | custom-call | tf_op jit(solution)/shard_map/pallas_call | solution.py:913
  (8 shorter events, 0.1 us)
Async XLA Ops:
  0.0 2.0 %copy-start = (s32[2048,6]{0,1:T(8,128)S(1)}, s32[2048,6]{0,1:T(8,128)}, u32[]{:S(2)}) copy-start(s32[2048,6]{0,1:T(8,128)} %param.4) | copy-start | bytes 147460
  1.2 117.8 %copy-start.2 = (s32[16]{0:T(128)}, s32[16]{0:T(128)S(1)}, u32[]{:S(2)}) copy-start(s32[16]{0:T(128)S(1)} %get-tuple-element.9.back) | copy-start | bytes 196
  3.2 2.7 %copy-start.1 = (s32[96]{0:T(128)}, s32[96]{0:T(128)S(1)}, u32[]{:S(2)}) copy-start(s32[96]{0:T(128)S(1)} %convert_reduce_fusion.refs_3_) | copy-start | bytes 1156

commit v3 on v2

--- a/solution.py
+++ b/solution.py
@@ -12,6 +12,12 @@
 BIT_OF = (4, 2, 1)
 TANGENT = ((2, 1), (1, 4), (2, 4))
 F32 = jnp.float32
+
+
+def send_order():
+    offsets = [(z, x, y) for z in range(8) for x in range(4) for y in range(4)][1:]
+    mixed = [offsets[(53 * k + 26) % 127] for k in range(127)]
+    return sorted(mixed, key=lambda o: -(min(o[0], 8 - o[0]) + min(o[1], 4 - o[1]) + min(o[2], 4 - o[2])))
 
 
 def iota(axis):
@@ -264,43 +270,97 @@
     lax.fori_loop(0, 4, body, 0)
 
 
+def squeeze(tiles):
+    group = iota(1) // 32
+    rows = flip8(tiles)
+    pair = []
+    for r in range(2):
+        row = rows[4 * r]
+        for g in range(1, 4):
+            row = jnp.where(group == g, rows[4 * r + g], row)
+        pair.append(row)
+    return flip8(pair * 4)
+
+
+def unsqueeze(tiles, second):
+    rows = flip8([jnp.concatenate([tile, tile], axis=0) for tile in tiles])
+    pair = [jnp.where(second, rows[2 + r], rows[r]) for r in range(2)]
+    return flip8([pair[0]] * 4 + [pair[1]] * 4)
+
+
+def last_tiles(tiles):
+    lane = iota(1)
+    result = tiles[0:4]
+    for g in range(1, 4):
+        result = [jnp.where(lane % 4 == g, tiles[4 * g + m], result[m]) for m in range(4)]
+    return result
+
+
 def make_rims(V, items):
     def x_body(n, carry):
         s = n // 2
         t = n % 2
-        codes = [[V[0, c, 15 * s, 2 * h + t] for h in range(2)] for c in range(5)]
-        last = [half for tile in codes[4] for half in halves(tile)]
-        for g, tiles in enumerate((codes[0] + codes[1] + codes[2] + codes[3], last * 2)):
-            rows = flip8(tiles)
-            for j in range(8):
-                items[s * 16 + 8 * t + j, g] = rows[j]
+        codes = [V[0, c, 15 * s, 2 * h + t] for c in range(5) for h in range(2)]
+        rows = flip8(codes[:8])
+        last = flip8(codes[8:] * 4)
+        for j in range(8):
+            item = s * 16 + 8 * t + j
+            items[item, 0] = rows[j, 0:4]
+            items[item, 1] = rows[j, 4:8]
+            items[item, 2] = last[j, 0:4]
         return carry
 
     def body(n, carry):
         a = 1 + n // 2
         s = n % 2
         codes = [[V[a, c, 15 * s, k] for k in range(4)] for c in range(5)]
-        for g, tiles in enumerate((codes[0] + codes[1] + codes[2] + codes[3], codes[4] * 4)):
-            tiles = turn(tiles)
-            for q in range(16):
-                items[(2 + n) * 16 + q, g] = tiles[q]
+        store_rims(items, (2 + n) * 16, codes, range(16))
         return carry
 
     lax.fori_loop(0, 4, x_body, 0)
     lax.fori_loop(0, 4, body, 0)
 
 
-def pack(items, slots, send):
-    whole = items.shape[1] - 1
-
+def store_rims(items, first, codes, blocks):
+    tiles = turn(codes[0] + codes[1] + codes[2] + codes[3])
+    last = turn(codes[4] * 4)
+    for t in range(2):
+        pairs = squeeze(last[8 * t : 8 * t + 8])
+        for j in range(8):
+            q = 8 * t + j
+            if q in blocks:
+                items[first + q, 0] = tiles[q][0:4]
+                items[first + q, 1] = tiles[q][4:8]
+                items[first + q, 2] = pairs[j, 0:4]
+
+
+def rim_tile(recv, e, k):
+    return jnp.concatenate([recv[e, 2 * k], recv[e, 2 * k + 1]], axis=0)
+
+
+def pack_slabs(items, slots, send):
     def body(d, carry):
         lane = iota(1)
         i0 = slots[2 * d]
         i1 = slots[2 * d + 1]
-        for g in range(whole):
+        for g in range(2):
             send[d, g] = items[i0, g]
-            send[d, whole + g] = items[i1, g]
-        send[d, 2 * whole] = jnp.where(lane < 64, items[i0, whole], items[i1, whole])
+            send[d, 2 + g] = items[i1, g]
+        send[d, 4] = jnp.where(lane < 64, items[i0, 2], items[i1, 2])
+        return carry
+
+    lax.fori_loop(0, send.shape[0], body, 0)
+
+
+def pack_rims(items, slots, send):
+    def body(d, carry):
+        first = lax.broadcasted_iota(jnp.int32, (4, 128), 0) < 2
+        i0 = slots[2 * d]
+        i1 = slots[2 * d + 1]
+        for g in range(2):
+            send[d, g] = items[i0, g]
+            send[d, 2 + g] = items[i1, g]
+        send[d, 4] = jnp.where(first, items[i0, 2], items[i1, 2])
         return carry
 
     lax.fori_loop(0, send.shape[0], body, 0)
@@ -359,25 +419,29 @@
     lax.fori_loop(0, 5, body, 0)
 
 
-def late_rims(recv, where, which, lane_mask, rims):
+def late_rims(recv, where, which, row_mask, rims):
     for f in range(2):
         for t in range(2):
             item = f * 16 + 8 * t
             r = 4 * f + 2 * t
-            tile = recv[where[item], which[item]]
+            tile = rim_tile(recv, where[item], which[item])
             for c in range(4):
                 rims[20 + c, r : r + 2, :] = tile[2 * c : 2 * c + 2]
-            tile = recv[where[item], 2]
-            joined = join(tile, pltpu.roll(tile, 7, 0), which[item] == 1)
-            for h in range(2):
-                rims[24, r + h : r + h + 1, :] = joined[2 * h : 2 * h + 1]
+            tile = recv[where[item], 4]
+            rims[24, r : r + 2, :] = jnp.where(which[item] == 1, tile[2:4], tile[0:2])
     items = [f * 16 + 8 * t for t in range(2) for _ in range(2) for f in range(2, 6)]
-    tiles = turn([recv[where[i], which[i]] for i in items])
+    tiles = turn([rim_tile(recv, where[i], which[i]) for i in items])
     for m in range(16):
         rims[m] = tiles[m]
-    tiles = turn([recv[where[i], 2] for i in items])
+    tiles = []
+    for t in range(2):
+        rows = unsqueeze(
+            [recv[where[i], 4] for i in items[8 * t : 8 * t + 8]], row_mask[12 + t] > 0.5
+        )
+        tiles += [rows[j] for j in range(8)]
+    tiles = last_tiles(turn(tiles))
     for m in range(4):
-        rims[16 + m] = jnp.where(lane_mask[4] > 0.5, tiles[8 + m], tiles[m])
+        rims[16 + m] = tiles[m]
 
 
 def spread_rows(tile, u):
@@ -389,7 +453,30 @@
     return result
 
 
-def fine_ghosts(V, rims, G, late=None):
+def sibling_ghosts(V, G):
+    def x_body(c, carry):
+        for f in range(2):
+            for layer in range(2):
+                for k in range(4):
+                    near = V[0, c, (layer if f else 14 + layer), k]
+                    G[f, c, layer, k] = pltpu.roll(near, 4, 0)
+        return carry
+
+    def body(c, carry):
+        for f in range(2, 6):
+            a, s = f // 2, f % 2
+            by = (128 - 8 * BIT_OF[a]) if s else 8 * BIT_OF[a]
+            for layer in range(2):
+                for k in range(4):
+                    near = V[a, c, (layer if s else 14 + layer), k]
+                    G[f, c, layer, k] = pltpu.roll(near, by, 1)
+        return carry
+
+    lax.fori_loop(0, 5, x_body, 0)
+    lax.fori_loop(0, 5, body, 0)
+
+
+def coarse_ghosts(rims, G, late=None):
     lane = iota(1)
     sub = iota(0)
 
@@ -397,12 +484,11 @@
         value = rims[index]
         return value if late is None else 0.5 * (value + late[index])
 
-    for f in range(2):
-        outer = (sub // 4) % 2 == f
+    def x_body(c, carry):
         first = (sub // 2) % 2 == 1
         second = sub % 2
-
-        def x_body(c, carry):
+        for f in range(2):
+            outer = (sub // 4) % 2 == f
             for t in range(2):
                 r = 4 * f + 2 * t
                 row = [
@@ -414,23 +500,19 @@
                     index = (4 * h + lane // 32) * 16 + 8 * second + (lane % 16) // 2
                     coarse = take(source, index)
                     for layer in range(2):
-                        near = V[0, c, (layer if f else 14 + layer), 2 * h + t]
-                        near = pltpu.roll(near, 4, 0)
-                        G[f, c, layer, 2 * h + t] = jnp.where(outer, coarse, near)
-            return carry
-
-        lax.fori_loop(0, 5, x_body, 0)
+                        k = 2 * h + t
+                        G[f, c, layer, k] = jnp.where(outer, coarse, G[f, c, layer, k])
+        return carry
 
     octant = lane // 8 % 8
-    for f in range(2, 6):
-        a, s = f // 2, f % 2
-        bit = BIT_OF[a]
-        outer = octant // bit % 2 == s
-        first = octant // TANGENT[a][0] % 2 == 1
+
+    def body(c, carry):
+        source = [rim(4 * c + k) for k in range(4)]
         second = octant // 4 == 1
-
-        def body(c, carry):
-            source = [rim(4 * c + k) for k in range(4)]
+        for f in range(2, 6):
+            a, s = f // 2, f % 2
+            outer = octant // BIT_OF[a] % 2 == s
+            first = octant // TANGENT[a][0] % 2 == 1
             for X in range(2):
                 index = (lane // 64 * 8 + f - 2) * 8 + 4 * X + lane % 8 // 2
                 four = [take(tile, index) for tile in source]
@@ -440,12 +522,12 @@
                 for u in range(2):
                     coarse = spread_rows(chosen, u)
                     for layer in range(2):
-                        near = V[a, c, (layer if s else 14 + layer), 2 * u + X]
-                        near = pltpu.roll(near, (128 - 8 * bit) if s else 8 * bit, 1)
-                        G[f, c, layer, 2 * u + X] = jnp.where(outer, coarse, near)
-            return carry
-
-        lax.fori_loop(0, 5, body, 0)
+                        k = 2 * u + X
+                        G[f, c, layer, k] = jnp.where(outer, coarse, G[f, c, layer, k])
+        return carry
+
+    lax.fori_loop(0, 5, x_body, 0)
+    lax.fori_loop(0, 5, body, 0)
 
 
 def pair_sums(low, high):
@@ -517,7 +599,6 @@
 
 
 def make_deltas(FC, means, items):
-    lane = lax.broadcasted_iota(jnp.int32, (1, 128), 1)
     for f in range(2):
         for t in range(2):
             item = f * 16 + 8 * t
@@ -526,25 +607,22 @@
                     r = 4 * f + 2 * t + h
                     delta = FC[f, c, 2 * h + t, 0:1, :] - means[20 + c, r : r + 1, :]
                     if c < 4:
-                        items[item, 0, 2 * c + h : 2 * c + h + 1, :] = delta
+                        row = 2 * (c % 2) + h
+                        items[item, c // 2, row : row + 1, :] = delta
                     else:
-                        other = pltpu.roll(delta, 64, 1)
-                        items[item, 1, 2 * h : 2 * h + 1, :] = jnp.where(lane < 64, delta, other)
-                        items[item, 1, 2 * h + 1 : 2 * h + 2, :] = jnp.where(
-                            lane < 64, other, delta
-                        )
+                        items[item, 2, h : h + 1, :] = delta
+                        items[item, 2, 2 + h : 3 + h, :] = delta
     for n in range(4):
         a, s = 1 + n // 2, n % 2
         codes = []
         for c in range(5):
             fine = means[5 * n + c]
+            codes.append([])
             for k in range(4):
                 o = s * BIT_OF[a] + (k // 2) * TANGENT[a][0] + (k % 2) * 4
-                codes.append(FC[2 + n, c, k] - pltpu.roll(fine, (128 - 8 * o) % 128, 1))
-        for g, tiles in enumerate((codes[:16], codes[16:] * 4)):
-            tiles = turn(tiles)
-            for t in range(2):
-                items[(2 + n) * 16 + 8 * t, g] = tiles[8 * t]
+                moved = pltpu.roll(fine, (128 - 8 * o) % 128, 1)
+                codes[c].append(FC[2 + n, c, k] - moved)
+        store_rims(items, (2 + n) * 16, codes, (0, 8))
 
 
 def take_mixed(N, mixed):
@@ -558,7 +636,7 @@
     lax.fori_loop(0, 5, body, 0)
 
 
-def apply_corrections(recv, where, which, lane_mask, change, N):
+def apply_corrections(recv, where, which, row_mask, change, N):
     sub = iota(0)
 
     def x_body(q, carry):
@@ -567,12 +645,12 @@
             item = s * 16 + q
             e = where[item]
             k = which[item]
-            tile = recv[e, 2]
-            joined = join(tile, pltpu.roll(tile, 7, 0), k == 1)
-            tile = recv[e, k]
+            tile = recv[e, 4]
+            last = jnp.where(k == 1, tile[2:4], tile[0:2])
+            tile = rim_tile(recv, e, k)
             for c in range(5):
                 for h in range(2):
-                    row = tile[2 * c + h : 2 * c + h + 1] if c < 4 else joined[2 * h : 2 * h + 1]
+                    row = tile[2 * c + h : 2 * c + h + 1] if c < 4 else last[h : h + 1]
                     row = jnp.broadcast_to(scale * row, (8, 128))
                     N[q, c, s, h] = N[q, c, s, h] + jnp.where(sub == 7 * s, row, 0.0)
         return carry
@@ -582,12 +660,19 @@
     for n in range(4):
         scale = RATIO if n % 2 else -RATIO
         first = (2 + n) * 16
-        tiles = turn([recv[where[first + q], which[first + q]] for q in range(16)])
+        tiles = turn([rim_tile(recv, where[first + q], which[first + q]) for q in range(16)])
         for m in range(16):
             change[n, m // 4, m % 4] = scale * tiles[m]
-        tiles = turn([recv[where[first + q], 2] for q in range(16)])
+        tiles = []
+        for t in range(2):
+            rows = unsqueeze(
+                [recv[where[first + 8 * t + j], 4] for j in range(8)],
+                row_mask[4 + 2 * n + t] > 0.5,
+            )
+            tiles += [rows[j] for j in range(8)]
+        tiles = last_tiles(turn(tiles))
         for m in range(4):
-            change[n, 4, m] = scale * jnp.where(lane_mask[n] > 0.5, tiles[8 + m], tiles[m])
+            change[n, 4, m] = scale * tiles[m]
 
     def body(X, carry):
         for c in range(5):
@@ -617,7 +702,7 @@
     slots,
     where,
     which,
-    fluid,
+    fluid_hbm,
     row_mask,
     lane_mask,
     out,
@@ -649,6 +734,8 @@
     pair_send,
     pair_recv,
     ready,
+    fluid,
+    load_sem,
 ):
     level = lax.axis_index("level")
     me = lax.axis_index("blk")
@@ -656,19 +743,16 @@
     barrier = pltpu.get_barrier_semaphore()
 
     def start_all(send, recv, n):
-        def body(k, carry):
-            d = lax.rem(k * 53 + 26, devices - 1)
+        for dz, dx, dy in send_order():
+            d = dz * 16 + dx * 4 + dy - 1
             pltpu.make_async_remote_copy(
                 src_ref=send.at[d],
                 dst_ref=recv.at[d],
                 send_sem=send_sems.at[n],
                 recv_sem=recv_sems.at[n],
-                device_id=(level, lax.rem(me + d + 1, devices)),
+                device_id=(level, far[dz] + mid[dx] + near[dy]),
                 device_id_type=MESH,
             ).start()
-            return carry
-
-        lax.fori_loop(0, devices - 1, body, 0)
 
     def whole(send, recv, n):
         return pltpu.make_async_remote_copy(
@@ -696,34 +780,35 @@
                 semaphore, inc=1, device_id=(level, peer), device_id_type=MESH
             )
 
-    plane = devices // 8
-    far, mid, near = me // plane, me // 4 % 4, me % 4
-    line_far = [lax.rem(far + i, 8) * plane + me % plane for i in range(1, 8)]
-    line_mid = [far * plane + lax.rem(mid + i, 4) * 4 + near for i in range(1, 4)]
-    line_near = [far * plane + mid * 4 + lax.rem(near + i, 4) for i in range(1, 4)]
+    far = [lax.rem(me // 16 + i, 8) * 16 for i in range(8)]
+    mid = [lax.rem(me // 4 % 4 + i, 4) * 4 for i in range(4)]
+    near = [lax.rem(me % 4 + i, 4) for i in range(4)]
+    line = [far[i] + mid[0] + near[0] for i in range(1, 8)]
+    plane = [far[0] + mid[i] + near[j] for i in range(4) for j in range(4) if i or j]
 
     pl.semaphore_signal(barrier, inc=1, device_id=(other, me), device_id_type=MESH)
 
     @pl.when(level == 0)
     def _():
-        greet(barrier, line_far + line_mid + line_near)
-
+        greet(barrier, line + plane)
+
+    copy = pltpu.make_async_copy(fluid_hbm, fluid, load_sem)
+    copy.start()
+    copy.wait()
     make_views(N, V, fluid, perm)
 
     @pl.when(level == 0)
     def _():
-        pl.semaphore_wait(barrier, 14)
-        greet(ready.at[0], line_far)
+        pl.semaphore_wait(barrier, 23)
+        greet(ready, line)
         make_slabs(V, items1)
-        pl.semaphore_wait(ready.at[0], 7)
-        greet(ready.at[1], line_mid)
-        pack(items1, slots, send1)
-        pl.semaphore_wait(ready.at[1], 3)
+        pack_slabs(items1, slots, send1)
+        pl.semaphore_wait(ready, 7)
         start_all(send1, recv1, 0)
 
         def clear(n, carry):
-            for g in range(2):
-                items3[n, g] = jnp.zeros((8, 128), F32)
+            for g in range(3):
+                items3[n, g] = jnp.zeros((4, 128), F32)
             return carry
 
         lax.fori_loop(0, 96, clear, 0)
@@ -743,8 +828,9 @@
 
     @pl.when(level == 1)
     def _():
+        sibling_ghosts(V, G)
         to_pair(early_out, early_in, 0).wait_recv()
-        fine_ghosts(V, early_in, G)
+        coarse_ghosts(early_in, G)
 
     outer_sweep(V, G, D, FC, True)
     update(N, D)
@@ -753,26 +839,27 @@
     @pl.when(level == 0)
     def _():
         make_rims(V, items2)
-        pack(items2, slots, send2)
+        pack_rims(items2, slots, send2)
         start_all(send2, recv2, 1)
         whole(send2, recv2, 1).wait_recv()
-        late_rims(recv2, where, which, lane_mask, late_out)
+        late_rims(recv2, where, which, row_mask, late_out)
         to_pair(late_out, late_in, 1).start()
 
         to_pair(means_out, means_in, 3).wait_recv()
         make_deltas(FC, means_in, items3)
-        pack(items3, slots, send3)
+        pack_rims(items3, slots, send3)
         start_all(send3, recv3, 2)
         to_pair(mixed_out, mixed_in, 2).wait_recv()
         take_mixed(N, mixed_in)
         whole(send3, recv3, 2).wait_recv()
-        apply_corrections(recv3, where, which, lane_mask, change, N)
+        apply_corrections(recv3, where, which, row_mask, change, N)
 
     @pl.when(level == 1)
     def _():
         inner_sweep(V, D)
+        sibling_ghosts(V, G)
         to_pair(late_out, late_in, 1).wait_recv()
-        fine_ghosts(V, early_in, G, late_in)
+        coarse_ghosts(early_in, G, late_in)
         outer_sweep(V, G, D, FC, False)
         restrict_faces(FC, means_out)
         to_pair(means_out, means_in, 3).start()
@@ -839,8 +926,9 @@
         axis=1,
         dtype=jnp.int32,
     )
-    to = (target - me + devices - 1) % devices
-    come = (me - target + devices - 1) % devices
+    far, mid, near = target // 16 - me // 16, target // 4 % 4 - me // 4 % 4, target % 4 - me % 4
+    to = (far % 8) * 16 + (mid % 4) * 4 + near % 4 - 1
+    come = (-far % 8) * 16 + (-mid % 4) * 4 + (-near) % 4 - 1
     item_ids = jnp.arange(6 * count, dtype=jnp.int32)
     slot_ids = jnp.arange(2 * devices, dtype=jnp.int32)
     slots = jnp.sum(
@@ -849,10 +937,10 @@
         dtype=jnp.int32,
     )
     second = which.astype(F32).reshape(6, count)
-    row_mask = jnp.broadcast_to(second[:2].reshape(4, 8, 1), (4, 8, 128))
-    late = jnp.concatenate([second[2:, 0], second[2:, 0], second[2:, 8], second[2:, 8]])
-    lanes = jnp.concatenate([second[2:], late[None]])
-    lane_mask = jnp.broadcast_to(jnp.repeat(lanes, 8, axis=1)[:, None, :], (5, 8, 128))
+    late = jnp.stack([second[2:, 0], second[2:, 0], second[2:, 8], second[2:, 8]])
+    rows = jnp.concatenate([second.reshape(12, 8), late.reshape(2, 8)])
+    row_mask = jnp.broadcast_to(rows[:, :, None], (14, 8, 128))
+    lane_mask = jnp.broadcast_to(jnp.repeat(second[2:], 8, axis=1)[:, None, :], (4, 8, 128))
     return inverse(place), place, slots, come, which, row_mask, lane_mask
 
 
@@ -874,7 +962,7 @@
     result = pl.pallas_call(
         step,
         out_shape=jax.ShapeDtypeStruct(fluid_state.shape[1:], F32),
-        in_specs=[smem] * 4 + [vmem] * 3,
+        in_specs=[smem] * 4 + [pl.BlockSpec(memory_space=pl.ANY)] + [vmem] * 2,
         out_specs=vmem,
         scratch_shapes=[
             pltpu.VMEM((16, 5, 2, 2, 8, 128), F32),
@@ -884,14 +972,14 @@
             pltpu.VMEM((6, 5, 4, 8, 128), F32),
             pltpu.VMEM((4, 5, 4, 8, 128), F32),
             pltpu.VMEM((96, 3, 8, 128), F32),
-            pltpu.VMEM((96, 2, 8, 128), F32),
-            pltpu.VMEM((96, 2, 8, 128), F32),
+            pltpu.VMEM((96, 3, 4, 128), F32),
+            pltpu.VMEM((96, 3, 4, 128), F32),
             pltpu.VMEM((peers, 5, 8, 128), F32),
             pltpu.VMEM((peers, 5, 8, 128), F32),
-            pltpu.VMEM((peers, 3, 8, 128), F32),
-            pltpu.VMEM((peers, 3, 8, 128), F32),
-            pltpu.VMEM((peers, 3, 8, 128), F32),
-            pltpu.VMEM((peers, 3, 8, 128), F32),
+            pltpu.VMEM((peers, 5, 4, 128), F32),
+            pltpu.VMEM((peers, 5, 4, 128), F32),
+            pltpu.VMEM((peers, 5, 4, 128), F32),
+            pltpu.VMEM((peers, 5, 4, 128), F32),
             pltpu.VMEM((25, 8, 128), F32),
             pltpu.VMEM((25, 8, 128), F32),
             pltpu.VMEM((25, 8, 128), F32),
@@ -904,7 +992,9 @@
             pltpu.SemaphoreType.DMA((3,)),
             pltpu.SemaphoreType.DMA((4,)),
             pltpu.SemaphoreType.DMA((4,)),
-            pltpu.SemaphoreType.REGULAR((2,)),
+            pltpu.SemaphoreType.REGULAR,
+            pltpu.VMEM(fluid_state.shape, F32),
+            pltpu.SemaphoreType.DMA,
         ],
         compiler_params=pltpu.CompilerParams(
             collective_id=0, has_side_effects=True, vmem_limit_bytes=60 * 1024 * 1024

time: 123 us -> 107 us (0.87)
  Pallas kernels: 116 us -> 101 us
    pallas_call x1, Pallas kernels: 113 us -> 98.1 us  [local(): pl.pallas_call(step, out_shape=jax.ShapeDtypeStruct(fluid_state.shape[1:]...]
where the time goes in v3:
time: 107 us
  Pallas kernels  101 us (94%)
  local copies, waits for them, and re-layouts  3.16 us (3%)
  other arithmetic  2.76 us (3%)
    pallas_call x1, Pallas kernels, local(): pl.pallas_call(step, out_shape=jax.ShapeDtypeStruct(fluid_state.shape[1:]...  98.1 us
    pallas_call x1, Pallas kernels, local(): pl.pallas_call(place_kernel, out_shape=jax.ShapeDtypeStruct(fluid_state.s...  2.55 us

profile of v3, /device:TPU:2, one launch (start us, length us, event | category | flops | bytes accessed | tf_op | source)
XLA Modules:
  0.0 106.6 jit_solution(15074756703102034701)
XLA Ops:
  0.0 0.0 copy-start
  0.0 0.8 constant_dynamic-slice_fusion.1
  0.8 0.1 fusion
  0.9 0.1 convert_reduce_fusion.1
  1.0 0.2 select_reduce_fusion.4
  1.2 0.0 copy-start.2
  1.2 0.6 select_reduce_fusion.2
  1.8 0.1 iota_compare_fusion.1
  1.9 0.1 mul.93
  2.0 0.0 copy-done
  2.0 0.1 constant_dynamic-slice_fusion
  2.1 0.2 select_reduce_fusion.1
  2.3 0.1 reshape.375
  2.3 0.6 fusion.25
  2.9 0.1 reshape.376
  3.0 0.2 convert_reduce_fusion.refs_3_
  3.2 0.0 copy-start.1
  3.2 0.6 select_reduce_fusion.refs_1_
  3.9 0.1 slice.26
  4.0 0.1 slice.27
  4.0 0.1 convert_element_type.22
  4.1 0.2 slice_reduce_fusion.1
  4.3 0.1 reshape.377
  4.4 0.1 convert_element_type.21
  4.5 0.1 broadcast_in_dim.107
  4.6 0.1 broadcast_in_dim.108
  4.7 0.6 broadcast_in_dim.109.refs_6_
  5.3 0.7 broadcast_in_dim.106.refs_5_
  6.0 0.0 copy-done.1
  6.0 98.1 %shard_map.37.source = f32[16,5,16,256]{3,2,1,0:T(8,128)} custom-call(s32[16]{0:T(128)} %get-tuple-element.17.refs_0_, s32[256]{0:T(256)} %select_reduce_fusion.refs_1_, s32[96]{0:T(128)} %get-tuple-element.7.refs_2_, s32[96]{0:T(128)} %copy-done.1, f32[1,16,5,16,256]{4,3,2,1,0:T(8,128)} %refs_4_.1, f32[14,8,128]{2,1,0:T(8,128)} %broadcast_in_dim.106.refs_5_, ...), custom_call_target="tpu_custom_call" | custom-call | tf_op jit(solution)/shard_map/pallas_call | solution.py:962
  104.1 0.0 copy-done.2
  104.1 2.6 %shard_map.38 = f32[1,16,5,16,256]{4,3,2,1,0:T(8,128)} custom-call(s32[16]{0:T(128)} %copy-done.2, f32[16,5,16,256]{3,2,1,0:T(8,128)} %shard_map.37.source), custom_call_target="tpu_custom_call" | custom-call | tf_op jit(solution)/shard_map/pallas_call | solution.py:1003
  (9 shorter events, 0.1 us)
Async XLA Ops:
  0.0 2.0 %copy-start = (s32[2048,6]{0,1:T(8,128)S(1)}, s32[2048,6]{0,1:T(8,128)}, u32[]{:S(2)}) copy-start(s32[2048,6]{0,1:T(8,128)} %param.4) | copy-start | bytes 147460
  1.2 102.9 %copy-start.2 = (s32[16]{0:T(128)}, s32[16]{0:T(128)S(1)}, u32[]{:S(2)}) copy-start(s32[16]{0:T(128)S(1)} %get-tuple-element.12.back) | copy-start | bytes 196
  3.2 2.8 %copy-start.1 = (s32[96]{0:T(128)}, s32[96]{0:T(128)S(1)}, u32[]{:S(2)}) copy-start(s32[96]{0:T(128)S(1)} %convert_reduce_fusion.refs_3_) | copy-start | bytes 1156

commit v4 on v3

--- a/solution.py
+++ b/solution.py
@@ -400,20 +400,30 @@
     lax.fori_loop(0, 4, body, 0)
 
 
-def early_rims(G, rims):
+def parent_layers(read, out):
     face = iota(1) // 8 % 8
 
     def body(c, carry):
         for k in range(4):
-            tile = G[2, c, 1, k]
+            tile = read(2, c, k)
             for n in range(1, 4):
-                tile = jnp.where(face == n, pltpu.roll(G[2 + n, c, 1 - n % 2, k], 8 * n, 1), tile)
-            rims[4 * c + k] = tile
+                tile = jnp.where(face == n, pltpu.roll(read(2 + n, c, k), 8 * n, 1), tile)
+            out[4 * c + k] = tile
         for f in range(2):
             for t in range(2):
                 for h in range(2):
                     r = 4 * f + 2 * t + h
-                    rims[20 + c, r : r + 1, :] = G[f, c, 1 - f, 2 * h + t, 0:1, :]
+                    out[20 + c, r : r + 1, :] = read(f, c, 2 * h + t)[0:1]
+        return carry
+
+    lax.fori_loop(0, 5, body, 0)
+
+
+def part_layers(layers, out):
+    def body(c, carry):
+        for n in range(4):
+            for k in range(4):
+                out[n, c, k] = pltpu.roll(layers[4 * c + k], (128 - 8 * n) % 128, 1)
         return carry
 
     lax.fori_loop(0, 5, body, 0)
@@ -598,14 +608,14 @@
     lax.fori_loop(0, 5, body, 0)
 
 
-def make_deltas(FC, means, items):
+def make_deltas(layers, parted, means, items):
     for f in range(2):
         for t in range(2):
             item = f * 16 + 8 * t
             for c in range(5):
                 for h in range(2):
                     r = 4 * f + 2 * t + h
-                    delta = FC[f, c, 2 * h + t, 0:1, :] - means[20 + c, r : r + 1, :]
+                    delta = layers[20 + c, r : r + 1, :] - means[20 + c, r : r + 1, :]
                     if c < 4:
                         row = 2 * (c % 2) + h
                         items[item, c // 2, row : row + 1, :] = delta
@@ -621,7 +631,7 @@
             for k in range(4):
                 o = s * BIT_OF[a] + (k // 2) * TANGENT[a][0] + (k % 2) * 4
                 moved = pltpu.roll(fine, (128 - 8 * o) % 128, 1)
-                codes[c].append(FC[2 + n, c, k] - moved)
+                codes[c].append(parted[n, c, k] - moved)
         store_rims(items, (2 + n) * 16, codes, (0, 8))
 
 
@@ -723,12 +733,12 @@
     recv3,
     early_out,
     early_in,
-    late_out,
-    late_in,
+    faces_out,
+    faces_in,
     mixed_out,
     mixed_in,
-    means_out,
-    means_in,
+    late,
+    means,
     send_sems,
     recv_sems,
     pair_send,
@@ -742,7 +752,7 @@
     other = 1 - level
     barrier = pltpu.get_barrier_semaphore()
 
-    def start_all(send, recv, n):
+    def start_all(send, recv, n, target):
         for dz, dx, dy in send_order():
             d = dz * 16 + dx * 4 + dy - 1
             pltpu.make_async_remote_copy(
@@ -750,7 +760,7 @@
                 dst_ref=recv.at[d],
                 send_sem=send_sems.at[n],
                 recv_sem=recv_sems.at[n],
-                device_id=(level, far[dz] + mid[dx] + near[dy]),
+                device_id=(target, far[dz] + mid[dx] + near[dy]),
                 device_id_type=MESH,
             ).start()
 
@@ -804,7 +814,11 @@
         make_slabs(V, items1)
         pack_slabs(items1, slots, send1)
         pl.semaphore_wait(ready, 7)
-        start_all(send1, recv1, 0)
+        start_all(send1, recv1, 0, 0)
+
+    @pl.when(level == 1)
+    def _():
+        pl.semaphore_wait(barrier, 1)
 
         def clear(n, carry):
             for g in range(3):
@@ -813,17 +827,13 @@
 
         lax.fori_loop(0, 96, clear, 0)
 
-    @pl.when(level == 1)
-    def _():
-        pl.semaphore_wait(barrier, 1)
-
     inner_sweep(V, D)
 
     @pl.when(level == 0)
     def _():
         whole(send1, recv1, 0).wait_recv()
         collect_slabs(recv1, where, which, row_mask, lane_mask, G)
-        early_rims(G, early_out)
+        parent_layers(lambda f, c, k: G[f, c, 1 - f % 2, k], early_out)
         to_pair(early_out, early_in, 0).start()
 
     @pl.when(level == 1)
@@ -840,15 +850,9 @@
     def _():
         make_rims(V, items2)
         pack_rims(items2, slots, send2)
-        start_all(send2, recv2, 1)
-        whole(send2, recv2, 1).wait_recv()
-        late_rims(recv2, where, which, row_mask, late_out)
-        to_pair(late_out, late_in, 1).start()
-
-        to_pair(means_out, means_in, 3).wait_recv()
-        make_deltas(FC, means_in, items3)
-        pack_rims(items3, slots, send3)
-        start_all(send3, recv3, 2)
+        start_all(send2, recv2, 1, 1)
+        parent_layers(lambda f, c, k: FC[f, c, k], faces_out)
+        to_pair(faces_out, faces_in, 1).start()
         to_pair(mixed_out, mixed_in, 2).wait_recv()
         take_mixed(N, mixed_in)
         whole(send3, recv3, 2).wait_recv()
@@ -858,11 +862,16 @@
     def _():
         inner_sweep(V, D)
         sibling_ghosts(V, G)
-        to_pair(late_out, late_in, 1).wait_recv()
-        coarse_ghosts(early_in, G, late_in)
+        to_pair(faces_out, faces_in, 1).wait_recv()
+        part_layers(faces_in, change)
+        whole(send2, recv2, 1).wait_recv()
+        late_rims(recv2, where, which, row_mask, late)
+        coarse_ghosts(early_in, G, late)
         outer_sweep(V, G, D, FC, False)
-        restrict_faces(FC, means_out)
-        to_pair(means_out, means_in, 3).start()
+        restrict_faces(FC, means)
+        make_deltas(faces_in, change, means, items3)
+        pack_rims(items3, slots, send3)
+        start_all(send3, recv3, 2, 0)
         update(N, D)
         restrict_cells(N, mixed_out)
         to_pair(mixed_out, mixed_in, 2).start()
@@ -873,14 +882,13 @@
     def _():
         whole(send1, recv1, 0).wait_send()
         whole(send2, recv2, 1).wait_send()
-        whole(send3, recv3, 2).wait_send()
         to_pair(early_out, early_in, 0).wait_send()
-        to_pair(late_out, late_in, 1).wait_send()
+        to_pair(faces_out, faces_in, 1).wait_send()
 
     @pl.when(level == 1)
     def _():
+        whole(send3, recv3, 2).wait_send()
         to_pair(mixed_out, mixed_in, 2).wait_send()
-        to_pair(means_out, means_in, 3).wait_send()
 
 
 def place_kernel(back, source, out):
@@ -990,8 +998,8 @@
             pltpu.VMEM((25, 8, 128), F32),
             pltpu.SemaphoreType.DMA((3,)),
             pltpu.SemaphoreType.DMA((3,)),
-            pltpu.SemaphoreType.DMA((4,)),
-            pltpu.SemaphoreType.DMA((4,)),
+            pltpu.SemaphoreType.DMA((3,)),
+            pltpu.SemaphoreType.DMA((3,)),
             pltpu.SemaphoreType.REGULAR,
             pltpu.VMEM(fluid_state.shape, F32),
             pltpu.SemaphoreType.DMA,

time: 107 us -> 104 us (0.972)
  Pallas kernels: 101 us -> 97.6 us
    pallas_call x1, Pallas kernels: 98.1 us -> 95.1 us  [local(): pl.pallas_call(step, out_shape=jax.ShapeDtypeStruct(fluid_state.shape[1:]...]
where the time goes in v4:
time: 104 us
  Pallas kernels  97.6 us (94%)
  local copies, waits for them, and re-layouts  3.16 us (3%)
  other arithmetic  2.76 us (3%)
    pallas_call x1, Pallas kernels, local(): pl.pallas_call(step, out_shape=jax.ShapeDtypeStruct(fluid_state.shape[1:]...  95.1 us
    pallas_call x1, Pallas kernels, local(): pl.pallas_call(place_kernel, out_shape=jax.ShapeDtypeStruct(fluid_state.s...  2.55 us

profile of v4, /device:TPU:2, one launch (start us, length us, event | category | flops | bytes accessed | tf_op | source)
XLA Modules:
  0.0 103.6 jit_solution(10563872182440153360)
XLA Ops:
  0.0 0.0 copy-start
  0.0 0.8 constant_dynamic-slice_fusion.1
  0.8 0.1 fusion
  0.9 0.1 convert_reduce_fusion.1
  1.0 0.2 select_reduce_fusion.4
  1.2 0.0 copy-start.2
  1.2 0.6 select_reduce_fusion.2
  1.8 0.1 iota_compare_fusion.1
  1.9 0.1 mul.93
  2.0 0.0 copy-done
  2.0 0.1 constant_dynamic-slice_fusion
  2.1 0.2 select_reduce_fusion.1
  2.3 0.1 reshape.375
  2.3 0.6 fusion.25
  2.9 0.1 reshape.376
  3.0 0.2 convert_reduce_fusion.refs_3_
  3.2 0.0 copy-start.1
  3.2 0.6 select_reduce_fusion.refs_1_
  3.9 0.1 slice.26
  4.0 0.1 slice.27
  4.0 0.1 convert_element_type.22
  4.1 0.2 slice_reduce_fusion.1
  4.3 0.1 reshape.377
  4.4 0.1 convert_element_type.21
  4.5 0.1 broadcast_in_dim.107
  4.6 0.1 broadcast_in_dim.108
  4.7 0.6 broadcast_in_dim.109.refs_6_
  5.3 0.7 broadcast_in_dim.106.refs_5_
  6.0 0.0 copy-done.1
  6.0 95.1 %shard_map.37.source = f32[16,5,16,256]{3,2,1,0:T(8,128)} custom-call(s32[16]{0:T(128)} %get-tuple-element.17.refs_0_, s32[256]{0:T(256)} %select_reduce_fusion.refs_1_, s32[96]{0:T(128)} %get-tuple-element.7.refs_2_, s32[96]{0:T(128)} %copy-done.1, f32[1,16,5,16,256]{4,3,2,1,0:T(8,128)} %refs_4_.1, f32[14,8,128]{2,1,0:T(8,128)} %broadcast_in_dim.106.refs_5_, ...), custom_call_target="tpu_custom_call" | custom-call | tf_op jit(solution)/shard_map/pallas_call | solution.py:970
  101.1 0.0 copy-done.2
  101.1 2.6 %shard_map.38 = f32[1,16,5,16,256]{4,3,2,1,0:T(8,128)} custom-call(s32[16]{0:T(128)} %copy-done.2, f32[16,5,16,256]{3,2,1,0:T(8,128)} %shard_map.37.source), custom_call_target="tpu_custom_call" | custom-call | tf_op jit(solution)/shard_map/pallas_call | solution.py:1011
  (9 shorter events, 0.1 us)
Async XLA Ops:
  0.0 2.0 %copy-start = (s32[2048,6]{0,1:T(8,128)S(1)}, s32[2048,6]{0,1:T(8,128)}, u32[]{:S(2)}) copy-start(s32[2048,6]{0,1:T(8,128)} %param.4) | copy-start | bytes 147460
  1.2 99.9 %copy-start.2 = (s32[16]{0:T(128)}, s32[16]{0:T(128)S(1)}, u32[]{:S(2)}) copy-start(s32[16]{0:T(128)S(1)} %get-tuple-element.12.back) | copy-start | bytes 196
  3.2 2.8 %copy-start.1 = (s32[96]{0:T(128)}, s32[96]{0:T(128)S(1)}, u32[]{:S(2)}) copy-start(s32[96]{0:T(128)S(1)} %convert_reduce_fusion.refs_3_) | copy-start | bytes 1156

commit v5 on v4

--- a/solution.py
+++ b/solution.py
@@ -338,8 +338,19 @@
     return jnp.concatenate([recv[e, 2 * k], recv[e, 2 * k + 1]], axis=0)
 
 
+def pack_all(one, count):
+    def body(n, carry):
+        for i in range(4):
+            one(4 * n + i)
+        return carry
+
+    lax.fori_loop(0, count // 4, body, 0)
+    for d in range(count // 4 * 4, count):
+        one(d)
+
+
 def pack_slabs(items, slots, send):
-    def body(d, carry):
+    def one(d):
         lane = iota(1)
         i0 = slots[2 * d]
         i1 = slots[2 * d + 1]
@@ -347,13 +358,12 @@
             send[d, g] = items[i0, g]
             send[d, 2 + g] = items[i1, g]
         send[d, 4] = jnp.where(lane < 64, items[i0, 2], items[i1, 2])
-        return carry
-
-    lax.fori_loop(0, send.shape[0], body, 0)
+
+    pack_all(one, send.shape[0])
 
 
 def pack_rims(items, slots, send):
-    def body(d, carry):
+    def one(d):
         first = lax.broadcasted_iota(jnp.int32, (4, 128), 0) < 2
         i0 = slots[2 * d]
         i1 = slots[2 * d + 1]
@@ -361,9 +371,8 @@
             send[d, g] = items[i0, g]
             send[d, 2 + g] = items[i1, g]
         send[d, 4] = jnp.where(first, items[i0, 2], items[i1, 2])
-        return carry
-
-    lax.fori_loop(0, send.shape[0], body, 0)
+
+    pack_all(one, send.shape[0])
 
 
 def collect_slabs(recv, where, which, row_mask, lane_mask, G):
@@ -398,6 +407,33 @@
 
     lax.fori_loop(0, 4, x_body, 0)
     lax.fori_loop(0, 4, body, 0)
+
+
+def make_masks(which, row_mask, lane_mask):
+    def value(item):
+        return which[item].astype(F32)
+
+    def row_body(n, carry):
+        mask = jnp.zeros((8, 128), F32)
+        for j in range(8):
+            mask = jnp.where(iota(0) == j, value(8 * n + j), mask)
+        row_mask[n] = mask
+        return carry
+
+    def lane_body(n, carry):
+        mask = jnp.zeros((8, 128), F32)
+        for q in range(16):
+            mask = jnp.where(iota(1) // 8 == q, value((2 + n) * 16 + q), mask)
+        lane_mask[n] = mask
+        return carry
+
+    lax.fori_loop(0, 12, row_body, 0)
+    lax.fori_loop(0, 4, lane_body, 0)
+    for t in range(2):
+        mask = jnp.zeros((8, 128), F32)
+        for j in range(8):
+            mask = jnp.where(iota(0) == j, value((2 + j % 4) * 16 + 8 * t), mask)
+        row_mask[12 + t] = mask
 
 
 def parent_layers(read, out):
@@ -540,14 +576,16 @@
     lax.fori_loop(0, 5, body, 0)
 
 
+def lane_pairs(low, high):
+    even = iota(1) % 2 == 0
+    return jnp.where(even, low + pltpu.roll(low, 127, 1), high + pltpu.roll(high, 1, 1))
+
+
 def pair_sums(low, high):
     lane = iota(1)
-    index = (lane // 16 % 4) * 32 + 2 * (lane % 8)
-    sums = []
-    for tile in (low, high):
-        tile = tile + pltpu.roll(tile, 127, 1)
-        sums.append(take(tile + pltpu.roll(tile, 112, 1), index))
-    merged = jnp.where(lane < 64, sums[0], sums[1])
+    index = (lane // 16 % 4) * 32 + 2 * (lane % 8) + lane // 64
+    pairs = lane_pairs(low, high)
+    merged = take(pairs + pltpu.roll(pairs, 112, 1), index)
     return jnp.where(lane % 16 < 8, merged, pltpu.roll(merged, 7, 0))
 
 
@@ -574,7 +612,17 @@
     lane = iota(1)
     sub = iota(0)
 
-    def x_body(c, carry):
+    def body(c, carry):
+        index = lane // 8 * 8 + 2 * (lane % 4) + lane // 4 % 2
+        for n in range(4):
+            result = None
+            for u in range(2):
+                pairs = lane_pairs(FC[2 + n, c, 2 * u], FC[2 + n, c, 2 * u + 1])
+                merged = take(pairs + pltpu.roll(pairs, 7, 0), index)
+                for i in range(4):
+                    moved = pltpu.roll(merged, ((4 if u else 8) - i) % 8, 0)
+                    result = moved if result is None else jnp.where(sub == 4 * u + i, moved, result)
+            means[5 * n + c] = result * 0.125
         for f in range(2):
             for t in range(2):
                 merged = pair_sums(FC[f, c, t], FC[f, c, 2 + t]) * 0.125
@@ -584,27 +632,6 @@
                     means[20 + c, r : r + 1, :] = merged[o : o + 1]
         return carry
 
-    def body(c, carry):
-        index = lane // 8 * 8 + 2 * (lane % 4)
-        for n in range(4):
-            result = None
-            for u in range(2):
-                sums = []
-                for X in range(2):
-                    tile = FC[2 + n, c, 2 * u + X]
-                    tile = tile + pltpu.roll(tile, 127, 1)
-                    sums.append(take(tile + pltpu.roll(tile, 7, 0), index))
-                merged = jnp.where(lane % 8 < 4, sums[0], sums[1])
-                for i in range(4):
-                    moved = pltpu.roll(merged, (8 - i) % 8, 0) if u == 0 else pltpu.roll(merged, 4 - i, 0)
-                    if result is None:
-                        result = moved
-                    else:
-                        result = jnp.where(sub == 4 * u + i, moved, result)
-            means[5 * n + c] = result * 0.125
-        return carry
-
-    lax.fori_loop(0, 5, x_body, 0)
     lax.fori_loop(0, 5, body, 0)
 
 
@@ -713,8 +740,6 @@
     where,
     which,
     fluid_hbm,
-    row_mask,
-    lane_mask,
     out,
     N,
     V,
@@ -744,6 +769,8 @@
     pair_send,
     pair_recv,
     ready,
+    row_mask,
+    lane_mask,
     fluid,
     load_sem,
 ):
@@ -828,13 +855,12 @@
         lax.fori_loop(0, 96, clear, 0)
 
     inner_sweep(V, D)
+    make_masks(which, row_mask, lane_mask)
 
     @pl.when(level == 0)
     def _():
         whole(send1, recv1, 0).wait_recv()
         collect_slabs(recv1, where, which, row_mask, lane_mask, G)
-        parent_layers(lambda f, c, k: G[f, c, 1 - f % 2, k], early_out)
-        to_pair(early_out, early_in, 0).start()
 
     @pl.when(level == 1)
     def _():
@@ -850,6 +876,8 @@
     def _():
         make_rims(V, items2)
         pack_rims(items2, slots, send2)
+        parent_layers(lambda f, c, k: G[f, c, 1 - f % 2, k], early_out)
+        to_pair(early_out, early_in, 0).start()
         start_all(send2, recv2, 1, 1)
         parent_layers(lambda f, c, k: FC[f, c, k], faces_out)
         to_pair(faces_out, faces_in, 1).start()
@@ -891,12 +919,15 @@
         to_pair(mixed_out, mixed_in, 2).wait_send()
 
 
-def place_kernel(back, source, out):
-    def body(b, carry):
-        out[0, b] = source[back[b]]
-        return carry
-
-    lax.fori_loop(0, out.shape[1], body, 0)
+def place_kernel(back, source, out, sems):
+    copies = [
+        pltpu.make_async_copy(source.at[back[b]], out.at[0, b], sems.at[b])
+        for b in range(out.shape[1])
+    ]
+    for copy in copies:
+        copy.start()
+    for copy in copies:
+        copy.wait()
 
 
 def tables(neighbours, parents, level, me, count, devices):
@@ -944,12 +975,7 @@
         axis=1,
         dtype=jnp.int32,
     )
-    second = which.astype(F32).reshape(6, count)
-    late = jnp.stack([second[2:, 0], second[2:, 0], second[2:, 8], second[2:, 8]])
-    rows = jnp.concatenate([second.reshape(12, 8), late.reshape(2, 8)])
-    row_mask = jnp.broadcast_to(rows[:, :, None], (14, 8, 128))
-    lane_mask = jnp.broadcast_to(jnp.repeat(second[2:], 8, axis=1)[:, None, :], (4, 8, 128))
-    return inverse(place), place, slots, come, which, row_mask, lane_mask
+    return inverse(place), place, slots, come, which
 
 
 def local(fluid_state, neighbours, parents):
@@ -957,7 +983,7 @@
     me = lax.axis_index("blk")
     devices = lax.axis_size("blk")
     count = fluid_state.shape[1]
-    perm, place, slots, where, which, row_mask, lane_mask = tables(
+    perm, place, slots, where, which = tables(
         neighbours, parents, level, me, count, devices
     )
     smem = pl.BlockSpec(memory_space=pltpu.SMEM)
@@ -970,7 +996,7 @@
     result = pl.pallas_call(
         step,
         out_shape=jax.ShapeDtypeStruct(fluid_state.shape[1:], F32),
-        in_specs=[smem] * 4 + [pl.BlockSpec(memory_space=pl.ANY)] + [vmem] * 2,
+        in_specs=[smem] * 4 + [pl.BlockSpec(memory_space=pltpu.HBM)],
         out_specs=vmem,
         scratch_shapes=[
             pltpu.VMEM((16, 5, 2, 2, 8, 128), F32),
@@ -1001,18 +1027,22 @@
             pltpu.SemaphoreType.DMA((3,)),
             pltpu.SemaphoreType.DMA((3,)),
             pltpu.SemaphoreType.REGULAR,
+            pltpu.VMEM((14, 8, 128), F32),
+            pltpu.VMEM((4, 8, 128), F32),
             pltpu.VMEM(fluid_state.shape, F32),
             pltpu.SemaphoreType.DMA,
         ],
         compiler_params=pltpu.CompilerParams(
-            collective_id=0, has_side_effects=True, vmem_limit_bytes=60 * 1024 * 1024
+            collective_id=0, has_side_effects=True, vmem_limit_bytes=34 * 1024 * 1024
         ),
-    )(perm, slots, where, which, fluid_state, row_mask, lane_mask)
+    )(perm, slots, where, which, fluid_state)
     return pl.pallas_call(
         place_kernel,
         out_shape=jax.ShapeDtypeStruct(fluid_state.shape, F32),
         in_specs=[smem, vmem],
-        out_specs=vmem,
+        out_specs=pl.BlockSpec(memory_space=pl.ANY),
+        scratch_shapes=[pltpu.SemaphoreType.DMA((count,))],
+        compiler_params=pltpu.CompilerParams(vmem_limit_bytes=8 * 1024 * 1024),
     )(place, result)
 
 

time: 104 us -> 97 us (0.933)
  Pallas kernels: 97.6 us -> 93.3 us
  other arithmetic: 2.76 us -> 1.14 us
    pallas_call x1, Pallas kernels: 95.1 us -> 91.5 us  [local(): pl.pallas_call(step, out_shape=jax.ShapeDtypeStruct(fluid_state.shape[1:]...]
    broadcast_in_dim x4 -> x0, local copies, waits for them, and re-layouts: 1.48 us -> none  [the longest x1 0.7 us: tables(): row_mask = jnp.broadcast_to(rows[:, :, None], (14, 8, 128))]
    unnamed x6 -> x4, local copies, waits for them, and re-layouts: 0.01 us -> 1.32 us
where the time goes in v5:
time: 97 us; the launch traced here: 96.9 us
  Pallas kernels  93.3 us (96%)
  local copies, waits for them, and re-layouts  2.41 us (2%)
  other arithmetic  1.14 us (1%)
    pallas_call x1, Pallas kernels, local(): pl.pallas_call(step, out_shape=jax.ShapeDtypeStruct(fluid_state.shape[1:]...  91.5 us

profile of v5, /device:TPU:2, one launch (start us, length us, event | category | flops | bytes accessed | tf_op | source)
XLA Modules:
  0.0 96.9 jit_solution(3540976499076151573)
XLA Ops:
  0.0 0.0 copy-start
  0.0 0.8 constant_dynamic-slice_fusion.1
  0.8 0.1 fusion
  0.9 0.1 convert_reduce_fusion.1
  1.0 0.2 select_reduce_fusion.4
  1.2 0.1 select_reduce_fusion.2
  1.3 0.1 iota_compare_fusion.1
  1.4 0.1 mul.93
  1.5 0.0 copy-done
  1.5 0.1 constant_dynamic-slice_fusion
  1.6 0.2 select_reduce_fusion.1
  1.7 0.1 reshape.361
  1.9 0.1 reshape.362
  2.0 0.2 convert_reduce_fusion.refs_3_
  2.2 0.1 select_reduce_fusion.refs_1_
  2.3 0.0 copy-start.1
  2.3 1.3 %copy-done.1 = f32[1,16,5,16,256]{4,3,2,1,0:T(8,128)S(1)} copy-done((f32[1,16,5,16,256]{4,3,2,1,0:T(8,128)S(1)}, f32[1,16,5,16,256]{4,3,2,1,0:T(8,128)}, u32[]{:S(2)}) %copy-start.1) | copy-done | bytes 1310744
  3.6 91.5 %shard_map.37.source = f32[16,5,16,256]{3,2,1,0:T(8,128)S(1)} custom-call(s32[16]{0:T(128)S(1)} %get-tuple-element.13.refs_0_, s32[256]{0:T(256)S(1)} %select_reduce_fusion.refs_1_, s32[96]{0:T(128)S(1)} %get-tuple-element.5.refs_2_, s32[96]{0:T(128)S(1)} %convert_reduce_fusion.refs_3_, f32[1,16,5,16,256]{4,3,2,1,0:T(8,128)S(1)} %copy-done.1), custom_call_target="tpu_custom_call" | custom-call | tf_op jit(solution)/shard_map/pallas_call | solution.py:996
  95.1 1.7 %shard_map.38 = f32[1,16,5,16,256]{4,3,2,1,0:T(8,128)} custom-call(s32[16]{0:T(128)S(1)} %get-tuple-element.10.back, f32[16,5,16,256]{3,2,1,0:T(8,128)S(1)} %shard_map.37.source), custom_call_target="tpu_custom_call" | custom-call | tf_op jit(solution)/shard_map/pallas_call | solution.py:1039
  (8 shorter events, 0.1 us)
Async XLA Ops:
  0.0 1.5 %copy-start = (s32[2048,6]{0,1:T(8,128)S(1)}, s32[2048,6]{0,1:T(8,128)}, u32[]{:S(2)}) copy-start(s32[2048,6]{0,1:T(8,128)} %param.4) | copy-start | bytes 147460
  2.3 1.3 %copy-start.1 = (f32[1,16,5,16,256]{4,3,2,1,0:T(8,128)S(1)}, f32[1,16,5,16,256]{4,3,2,1,0:T(8,128)}, u32[]{:S(2)}) copy-start(f32[1,16,5,16,256]{4,3,2,1,0:T(8,128)} %refs_4_.1) | copy-start | bytes 3932164

commit v6 on v5

--- a/solution.py
+++ b/solution.py
@@ -22,6 +22,10 @@
 
 def iota(axis):
     return lax.broadcasted_iota(jnp.int32, (8, 128), axis)
+
+
+def in_one(count, first, second):
+    lax.fori_loop(0, count, lambda n, carry: second(n, first(n, carry)), 0)
 
 
 def take(tile, index):
@@ -144,7 +148,7 @@
     lax.fori_loop(0, 12, body, 0)
 
 
-def outer_sweep(V, G, D, FC, first):
+def outer_sweep(V, G, D, FC=None):
     def body(n, carry):
         a = n // 4
         ch = n % 4
@@ -158,7 +162,8 @@
         for c in range(5):
             D[a, c, 0, ch] = f1[c] - f0[c]
             D[a, c, 1, ch] = D[a, c, 1, ch] - f1[c]
-            FC[2 * a, c, ch] = f0[c] if first else FC[2 * a, c, ch] + f0[c]
+            if FC is not None:
+                FC[2 * a, c, ch] = f0[c]
         u = [cells(V, a, i, ch) for i in (13, 14, 15)]
         g = [ghost(G, a, 1, layer, ch) for layer in range(2)]
         _, r0 = half_step(u[0], u[1], u[2], low_wanted=False)
@@ -169,7 +174,30 @@
         for c in range(5):
             D[a, c, 14, ch] = D[a, c, 14, ch] + f0[c]
             D[a, c, 15, ch] = f1[c] - f0[c]
-            FC[2 * a + 1, c, ch] = f1[c] if first else FC[2 * a + 1, c, ch] + f1[c]
+            if FC is not None:
+                FC[2 * a + 1, c, ch] = f1[c]
+        return carry
+
+    lax.fori_loop(0, 12, body, 0)
+
+
+def edge_faces(V, G, FC):
+    def body(n, carry):
+        a = n // 4
+        ch = n % 4
+        u = [cells(V, a, i, ch) for i in range(2)]
+        g = [ghost(G, a, 0, layer, ch) for layer in range(2)]
+        _, high = half_step(g[0], g[1], u[0], low_wanted=False)
+        low, _ = half_step(g[1], u[0], u[1], high_wanted=False)
+        first = contact_flux(high, low)
+        u = [cells(V, a, i, ch) for i in (14, 15)]
+        g = [ghost(G, a, 1, layer, ch) for layer in range(2)]
+        _, high = half_step(u[0], u[1], g[0], low_wanted=False)
+        low, _ = half_step(u[1], g[0], g[1], high_wanted=False)
+        last = contact_flux(high, low)
+        for c in range(5):
+            FC[2 * a, c, ch] = FC[2 * a, c, ch] + first[c]
+            FC[2 * a + 1, c, ch] = FC[2 * a + 1, c, ch] + last[c]
         return carry
 
     lax.fori_loop(0, 12, body, 0)
@@ -266,8 +294,7 @@
                 items[(2 + n) * 16 + q, g] = tiles[q]
         return carry
 
-    lax.fori_loop(0, 4, x_body, 0)
-    lax.fori_loop(0, 4, body, 0)
+    in_one(4, x_body, body)
 
 
 def squeeze(tiles):
@@ -317,8 +344,7 @@
         store_rims(items, (2 + n) * 16, codes, range(16))
         return carry
 
-    lax.fori_loop(0, 4, x_body, 0)
-    lax.fori_loop(0, 4, body, 0)
+    in_one(4, x_body, body)
 
 
 def store_rims(items, first, codes, blocks):
@@ -405,8 +431,7 @@
             G[2 + n, 4, m // 4, m % 4] = jnp.where(second, tiles[8 + m], tiles[m])
         return carry
 
-    lax.fori_loop(0, 4, x_body, 0)
-    lax.fori_loop(0, 4, body, 0)
+    in_one(4, x_body, body)
 
 
 def make_masks(which, row_mask, lane_mask):
@@ -518,8 +543,7 @@
                     G[f, c, layer, k] = pltpu.roll(near, by, 1)
         return carry
 
-    lax.fori_loop(0, 5, x_body, 0)
-    lax.fori_loop(0, 5, body, 0)
+    in_one(5, x_body, body)
 
 
 def coarse_ghosts(rims, G, late=None):
@@ -572,8 +596,7 @@
                         G[f, c, layer, k] = jnp.where(outer, coarse, G[f, c, layer, k])
         return carry
 
-    lax.fori_loop(0, 5, x_body, 0)
-    lax.fori_loop(0, 5, body, 0)
+    in_one(5, x_body, body)
 
 
 def lane_pairs(low, high):
@@ -868,7 +891,7 @@
         to_pair(early_out, early_in, 0).wait_recv()
         coarse_ghosts(early_in, G)
 
-    outer_sweep(V, G, D, FC, True)
+    outer_sweep(V, G, D, FC)
     update(N, D)
     make_views(N, V)
 
@@ -895,11 +918,12 @@
         whole(send2, recv2, 1).wait_recv()
         late_rims(recv2, where, which, row_mask, late)
         coarse_ghosts(early_in, G, late)
-        outer_sweep(V, G, D, FC, False)
+        edge_faces(V, G, FC)
         restrict_faces(FC, means)
         make_deltas(faces_in, change, means, items3)
         pack_rims(items3, slots, send3)
         start_all(send3, recv3, 2, 0)
+        outer_sweep(V, G, D)
         update(N, D)
         restrict_cells(N, mixed_out)
         to_pair(mixed_out, mixed_in, 2).start()

time: 97 us -> 95.7 us (0.987)
  Pallas kernels: 93.3 us -> 91.9 us
    pallas_call x1, Pallas kernels: 91.5 us -> 90.2 us  [local(): pl.pallas_call(step, out_shape=jax.ShapeDtypeStruct(fluid_state.shape[1:]...]
where the time goes in v6:
time: 95.7 us; the launch traced here: 95.5 us
  Pallas kernels  91.9 us (96%)
  local copies, waits for them, and re-layouts  2.41 us (3%)
  other arithmetic  1.14 us (1%)
    pallas_call x1, Pallas kernels, local(): pl.pallas_call(step, out_shape=jax.ShapeDtypeStruct(fluid_state.shape[1:]...  90.2 us

profile of v6, /device:TPU:2, one launch (start us, length us, event | category | flops | bytes accessed | tf_op | source)
XLA Modules:
  0.0 95.5 jit_solution(1185588365972897611)
XLA Ops:
  0.0 0.0 copy-start
  0.0 0.8 constant_dynamic-slice_fusion.1
  0.8 0.1 fusion
  0.9 0.1 convert_reduce_fusion.1
  1.0 0.2 select_reduce_fusion.4
  1.2 0.1 select_reduce_fusion.2
  1.3 0.1 iota_compare_fusion.1
  1.4 0.1 mul.93
  1.5 0.0 copy-done
  1.5 0.1 constant_dynamic-slice_fusion
  1.6 0.2 select_reduce_fusion.1
  1.7 0.1 reshape.361
  1.9 0.1 reshape.362
  2.0 0.2 convert_reduce_fusion.refs_3_
  2.2 0.1 select_reduce_fusion.refs_1_
  2.3 0.0 copy-start.1
  2.3 1.3 %copy-done.1 = f32[1,16,5,16,256]{4,3,2,1,0:T(8,128)S(1)} copy-done((f32[1,16,5,16,256]{4,3,2,1,0:T(8,128)S(1)}, f32[1,16,5,16,256]{4,3,2,1,0:T(8,128)}, u32[]{:S(2)}) %copy-start.1) | copy-done | bytes 1310744
  3.6 90.2 %shard_map.37.source = f32[16,5,16,256]{3,2,1,0:T(8,128)S(1)} custom-call(s32[16]{0:T(128)S(1)} %get-tuple-element.13.refs_0_, s32[256]{0:T(256)S(1)} %select_reduce_fusion.refs_1_, s32[96]{0:T(128)S(1)} %get-tuple-element.5.refs_2_, s32[96]{0:T(128)S(1)} %convert_reduce_fusion.refs_3_, f32[1,16,5,16,256]{4,3,2,1,0:T(8,128)S(1)} %copy-done.1), custom_call_target="tpu_custom_call" | custom-call | tf_op jit(solution)/shard_map/pallas_call | solution.py:1020
  93.8 1.7 %shard_map.38 = f32[1,16,5,16,256]{4,3,2,1,0:T(8,128)} custom-call(s32[16]{0:T(128)S(1)} %get-tuple-element.10.back, f32[16,5,16,256]{3,2,1,0:T(8,128)S(1)} %shard_map.37.source), custom_call_target="tpu_custom_call" | custom-call | tf_op jit(solution)/shard_map/pallas_call | solution.py:1063
  (8 shorter events, 0.1 us)
Async XLA Ops:
  0.0 1.5 %copy-start = (s32[2048,6]{0,1:T(8,128)S(1)}, s32[2048,6]{0,1:T(8,128)}, u32[]{:S(2)}) copy-start(s32[2048,6]{0,1:T(8,128)} %param.4) | copy-start | bytes 147460
  2.3 1.3 %copy-start.1 = (f32[1,16,5,16,256]{4,3,2,1,0:T(8,128)S(1)}, f32[1,16,5,16,256]{4,3,2,1,0:T(8,128)}, u32[]{:S(2)}) copy-start(f32[1,16,5,16,256]{4,3,2,1,0:T(8,128)} %refs_4_.1) | copy-start | bytes 3932164

commit v7 on v6

--- a/solution.py
+++ b/solution.py
@@ -203,7 +203,7 @@
     lax.fori_loop(0, 12, body, 0)
 
 
-def update(N, D):
+def update(N, D, V=None):
     def body(n, carry):
         X = n // 2
         h = n % 2
@@ -219,38 +219,41 @@
                 rows = flip8([D[0, c, 8 * X + i, 2 * h + t] for i in range(8)])
                 for j in range(8):
                     q = 8 * t + j
-                    N[q, c, X, h] = N[q, c, X, h] - RATIO * (tiles[q] + rows[j])
+                    tiles[q] = N[q, c, X, h] - RATIO * (tiles[q] + rows[j])
+                    N[q, c, X, h] = tiles[q]
+            if V is not None:
+                view_tiles(tiles, V, c, X, h)
         return carry
 
     lax.fori_loop(0, 4, body, 0)
 
 
-def make_views(N, V, fluid=None, perm=None):
+def view_tiles(tiles, V, c, X, h):
+    c1, c2 = ORDER[1].index(c), ORDER[2].index(c)
+    for t in range(2):
+        rows = flip8(tiles[8 * t : 8 * t + 8])
+        for i in range(8):
+            V[0, c, 8 * X + i, 2 * h + t] = rows[i]
+    tiles = turn(tiles)
+    for z in range(2):
+        for y in range(8):
+            V[1, c1, 8 * h + y, 2 * z + X] = tiles[2 * y + z]
+        rows = flip8([tiles[2 * y + z] for y in range(8)])
+        for i in range(8):
+            V[2, c2, 8 * z + i, 2 * h + X] = rows[i]
+
+
+def load_views(N, V, fluid, perm):
     def body(n, carry):
         X = n // 2
         h = n % 2
+        rows = pl.ds(pl.multiple_of(8 * X, 8), 8)
+        lanes = pl.ds(pl.multiple_of(128 * h, 128), 128)
         for c in range(5):
-            c1, c2 = ORDER[1].index(c), ORDER[2].index(c)
-            tiles = []
+            tiles = [fluid[0, perm[q], c, rows, lanes] for q in range(16)]
             for q in range(16):
-                if fluid is None:
-                    tiles.append(N[q, c, X, h])
-                else:
-                    rows = pl.ds(pl.multiple_of(8 * X, 8), 8)
-                    lanes = pl.ds(pl.multiple_of(128 * h, 128), 128)
-                    tiles.append(fluid[0, perm[q], c, rows, lanes])
-                    N[q, c, X, h] = tiles[q]
-            for t in range(2):
-                rows = flip8(tiles[8 * t : 8 * t + 8])
-                for i in range(8):
-                    V[0, c, 8 * X + i, 2 * h + t] = rows[i]
-            tiles = turn(tiles)
-            for z in range(2):
-                for y in range(8):
-                    V[1, c1, 8 * h + y, 2 * z + X] = tiles[2 * y + z]
-                rows = flip8([tiles[2 * y + z] for y in range(8)])
-                for i in range(8):
-                    V[2, c2, 8 * z + i, 2 * h + X] = rows[i]
+                N[q, c, X, h] = tiles[q]
+            view_tiles(tiles, V, c, X, h)
         return carry
 
     lax.fori_loop(0, 4, body, 0)
@@ -762,7 +765,7 @@
     slots,
     where,
     which,
-    fluid_hbm,
+    fluid,
     out,
     N,
     V,
@@ -794,8 +797,6 @@
     ready,
     row_mask,
     lane_mask,
-    fluid,
-    load_sem,
 ):
     level = lax.axis_index("level")
     me = lax.axis_index("blk")
@@ -852,10 +853,7 @@
     def _():
         greet(barrier, line + plane)
 
-    copy = pltpu.make_async_copy(fluid_hbm, fluid, load_sem)
-    copy.start()
-    copy.wait()
-    make_views(N, V, fluid, perm)
+    load_views(N, V, fluid, perm)
 
     @pl.when(level == 0)
     def _():
@@ -892,16 +890,15 @@
         coarse_ghosts(early_in, G)
 
     outer_sweep(V, G, D, FC)
-    update(N, D)
-    make_views(N, V)
+    update(N, D, V)
 
     @pl.when(level == 0)
     def _():
         make_rims(V, items2)
         pack_rims(items2, slots, send2)
+        start_all(send2, recv2, 1, 1)
         parent_layers(lambda f, c, k: G[f, c, 1 - f % 2, k], early_out)
         to_pair(early_out, early_in, 0).start()
-        start_all(send2, recv2, 1, 1)
         parent_layers(lambda f, c, k: FC[f, c, k], faces_out)
         to_pair(faces_out, faces_in, 1).start()
         to_pair(mixed_out, mixed_in, 2).wait_recv()
@@ -1020,7 +1017,7 @@
     result = pl.pallas_call(
         step,
         out_shape=jax.ShapeDtypeStruct(fluid_state.shape[1:], F32),
-        in_specs=[smem] * 4 + [pl.BlockSpec(memory_space=pltpu.HBM)],
+        in_specs=[smem] * 4 + [vmem],
         out_specs=vmem,
         scratch_shapes=[
             pltpu.VMEM((16, 5, 2, 2, 8, 128), F32),
@@ -1053,8 +1050,6 @@
             pltpu.SemaphoreType.REGULAR,
             pltpu.VMEM((14, 8, 128), F32),
             pltpu.VMEM((4, 8, 128), F32),
-            pltpu.VMEM(fluid_state.shape, F32),
-            pltpu.SemaphoreType.DMA,
         ],
         compiler_params=pltpu.CompilerParams(
             collective_id=0, has_side_effects=True, vmem_limit_bytes=34 * 1024 * 1024

time: 95.7 us -> 95.2 us (level)
  no operation moved by 1% of the time
where the time goes in v7:
time: 95.2 us; the launch traced here: 95.1 us
  Pallas kernels  91.5 us (96%)
  local copies, waits for them, and re-layouts  2.41 us (3%)
  other arithmetic  1.14 us (1%)
    pallas_call x1, Pallas kernels, local(): pl.pallas_call(step, out_shape=jax.ShapeDtypeStruct(fluid_state.shape[1:]...  89.8 us

profile of v7, /device:TPU:2, one launch (start us, length us, event | category | flops | bytes accessed | tf_op | source)
XLA Modules:
  0.0 95.1 jit_solution(4163648579560528434)
XLA Ops:
  0.0 0.0 copy-start
  0.0 0.8 constant_dynamic-slice_fusion.1
  0.8 0.1 fusion
  0.9 0.1 convert_reduce_fusion.1
  1.0 0.2 select_reduce_fusion.4
  1.2 0.1 select_reduce_fusion.2
  1.3 0.1 iota_compare_fusion.1
  1.4 0.1 mul.93
  1.5 0.0 copy-done
  1.5 0.1 constant_dynamic-slice_fusion
  1.6 0.2 select_reduce_fusion.1
  1.7 0.1 reshape.361
  1.9 0.1 reshape.362
  2.0 0.2 convert_reduce_fusion.refs_3_
  2.2 0.1 select_reduce_fusion.refs_1_
  2.3 0.0 copy-start.1
  2.3 1.3 %copy-done.1 = f32[1,16,5,16,256]{4,3,2,1,0:T(8,128)S(1)} copy-done((f32[1,16,5,16,256]{4,3,2,1,0:T(8,128)S(1)}, f32[1,16,5,16,256]{4,3,2,1,0:T(8,128)}, u32[]{:S(2)}) %copy-start.1) | copy-done | bytes 1310744
  3.6 89.8 %shard_map.37.source = f32[16,5,16,256]{3,2,1,0:T(8,128)S(1)} custom-call(s32[16]{0:T(128)S(1)} %get-tuple-element.13.refs_0_, s32[256]{0:T(256)S(1)} %select_reduce_fusion.refs_1_, s32[96]{0:T(128)S(1)} %get-tuple-element.5.refs_2_, s32[96]{0:T(128)S(1)} %convert_reduce_fusion.refs_3_, f32[1,16,5,16,256]{4,3,2,1,0:T(8,128)S(1)} %copy-done.1), custom_call_target="tpu_custom_call" | custom-call | tf_op jit(solution)/shard_map/pallas_call | solution.py:1017
  93.4 1.7 %shard_map.38 = f32[1,16,5,16,256]{4,3,2,1,0:T(8,128)} custom-call(s32[16]{0:T(128)S(1)} %get-tuple-element.10.back, f32[16,5,16,256]{3,2,1,0:T(8,128)S(1)} %shard_map.37.source), custom_call_target="tpu_custom_call" | custom-call | tf_op jit(solution)/shard_map/pallas_call | solution.py:1058
  (8 shorter events, 0.1 us)
Async XLA Ops:
  0.0 1.5 %copy-start = (s32[2048,6]{0,1:T(8,128)S(1)}, s32[2048,6]{0,1:T(8,128)}, u32[]{:S(2)}) copy-start(s32[2048,6]{0,1:T(8,128)} %param.4) | copy-start | bytes 147460
  2.3 1.3 %copy-start.1 = (f32[1,16,5,16,256]{4,3,2,1,0:T(8,128)S(1)}, f32[1,16,5,16,256]{4,3,2,1,0:T(8,128)}, u32[]{:S(2)}) copy-start(f32[1,16,5,16,256]{4,3,2,1,0:T(8,128)} %refs_4_.1) | copy-start | bytes 3932164
